TPU v7x, 128 devices: a whole 4x4x4 slice. The times are simulated.
128 devices in a mesh: client: 16 (over y_lo, x, core), unit: 8 (over z, y_hi).
Axes of the slice: x: 4, y: 4 (y_hi: 2, y_lo: 2; y = y_hi * 2 + y_lo), z: 4, core: 2. Of those that a mesh axis runs over, the one named last changes fastest.
Arguments:
- token_ids: int32 [256], replicated, may hold values from 0 to 65535
- embed_table: bfloat16 [65536, 4096], P(('client', 'unit')), may hold values from -6 to 6
- norm_gain: float32 [4096], replicated, may hold values from 0.5 to 1.5
- client_gate: bfloat16 [16, 4096, 7168], P('client', None, 'unit'), may hold values from -0.09375 to 0.09375
- client_up: bfloat16 [16, 4096, 7168], P('client', None, 'unit'), may hold values from -0.09375 to 0.09375
- ref_gate: bfloat16 [4096, 7168], P('client', 'unit'), may hold values from -0.09375 to 0.09375
- ref_up: bfloat16 [4096, 7168], P('client', 'unit'), may hold values from -0.09375 to 0.09375
Outputs:
- merged: float32 [7168, 256], P('unit')
- score: float32 [16, 7168], P('client', 'unit')
All inputs are finite; a program needn't handle non-finite values.
Results may differ from a plain program's by a relative error of at most 0.014.
Values may be sent and summed in bfloat16 or wider, within the bound.
A program may use at most 128 MiB of HBM per device.

v0:
```python
import jax
import jax.numpy as jnp
from jax import lax
from jax.sharding import PartitionSpec as P

sharpness = 40.0
block_cols = 2048


def split_up(shard, dim, count):
    before, after = (shard.shape[:dim], shard.shape[dim + 1 :])
    return jnp.moveaxis(shard.reshape(*before, count, -1, *after), dim, 0)


def summed_on_arrival(shard, axis, dim):
    count = lax.axis_size(axis)
    blocks = lax.all_to_all(split_up(shard, dim, count), axis, 0, 0, tiled=True)
    return jnp.sum(blocks, axis=0)


def sent_together(arrays, axis, dim, along):
    widths = [a.shape[along] for a in arrays]
    both = jnp.concatenate(arrays, axis=along)
    result = summed_on_arrival(both, axis, dim)
    return tuple(jnp.split(result, [sum(widths[:k]) for k in range(1, len(widths))], axis=along))


def laid_out(blocks, dim):
    dims = list(blocks.shape[1:])
    dims[dim] *= blocks.shape[0]
    return jnp.moveaxis(blocks, 0, dim).reshape(dims)


def copy_for_each(shard, axis):
    copies = jnp.broadcast_to(shard, (lax.axis_size(axis), *shard.shape))
    return lax.all_to_all(copies, axis, split_axis=0, concat_axis=0, tiled=True)


def gather_directly(shard, axis, dim):
    return laid_out(copy_for_each(shard, axis), dim)


def filled_up(lines, count):
    spare = -len(lines) % count
    return jnp.pad(lines, [(0, spare)] + [(0, 0)] * (lines.ndim - 1))


def sent_and_summed(shard, axis, dim):
    blocks = split_up(shard, dim, lax.axis_size(axis))
    arrived = lax.all_to_all(blocks, axis, split_axis=0, concat_axis=0, tiled=True)
    return arrived.astype(jnp.float32).sum(axis=0)


def nested_sum(shard, axes):
    lines = shard.reshape(-1, shard.shape[-1])
    padded = filled_up(lines, lax.axis_size(axes))
    whole = gather_directly(sent_and_summed(padded, axes, 0).astype(jnp.bfloat16), axes, 0)
    return lax.slice_in_dim(whole, 0, len(lines)).reshape(shard.shape).astype(jnp.float32)


def standardize(hidden):
    center = jnp.mean(hidden, axis=0, keepdims=True)
    shifted = hidden - center
    spread = jnp.sqrt(jnp.mean(shifted * shifted, axis=0, keepdims=True) + 1e-06)
    return (shifted / spread).astype(jnp.bfloat16)


def block_ranges(length):
    return [(offset, min(block_cols, length - offset)) for offset in range(0, length, block_cols)]


def rms_scaled(values, norm_gain):
    scale = lax.rsqrt(jnp.mean(values * values, axis=1, keepdims=True) + 1e-05)
    return (values * scale * norm_gain[None, :]).astype(jnp.bfloat16)


def body(token_ids, embed_table, norm_gain, client_gate, client_up, ref_gate, ref_up):
    rows_here = embed_table.shape[0]
    table_start = (
        lax.axis_index("client") * lax.axis_size("unit") + lax.axis_index("unit")
    ) * rows_here
    table_rows = table_start + jnp.arange(rows_here, dtype=jnp.int32)
    selector = (token_ids[:, None] == table_rows[None, :]).astype(jnp.bfloat16)
    partial_rows = jnp.dot(selector, embed_table, preferred_element_type=jnp.float32)
    embedded = lax.psum(partial_rows, ("client", "unit"))
    normed = rms_scaled(embedded, norm_gain)
    token_count = normed.shape[0]
    inverse_tokens = 1.0 / token_count
    gate_local = jnp.dot(normed, client_gate[0], preferred_element_type=jnp.float32)
    up_local = jnp.dot(normed, client_up[0], preferred_element_type=jnp.float32)
    client_std = standardize(jax.nn.silu(gate_local) * up_local)
    row_span = ref_gate.shape[0]
    normed_slice = lax.dynamic_slice_in_dim(
        normed, lax.axis_index("client") * row_span, row_span, 1
    )
    gate_part = jnp.dot(normed_slice, ref_gate, preferred_element_type=jnp.float32)
    up_part = jnp.dot(normed_slice, ref_up, preferred_element_type=jnp.float32)
    gate_share, up_share = sent_together((gate_part, up_part), "client", 1, 0)
    ref_piece = standardize(jax.nn.silu(gate_share) * up_share)
    ref_std = gather_directly(ref_piece, "client", 1)
    local_units = client_std.shape[1]
    segment = lax.all_gather(client_std, "unit", axis=1, tiled=True)
    numerator = jnp.zeros((local_units, token_count), jnp.float32)
    colsum = jnp.zeros((local_units,), jnp.float32)
    weighted = jnp.zeros((local_units,), jnp.float32)
    for offset, width in block_ranges(segment.shape[1]):
        columns = segment[:, offset : offset + width]
        correlation = (
            jnp.dot(columns.T, ref_std, preferred_element_type=jnp.float32) * inverse_tokens
        )
        weights = jnp.exp(sharpness * correlation)
        numerator = numerator + lax.dot_general(
            weights.astype(jnp.bfloat16),
            columns,
            (((0,), (1,)), ((), ())),
            preferred_element_type=jnp.float32,
        )
        colsum = colsum + jnp.sum(weights, axis=0)
        weighted = weighted + jnp.sum(weights * correlation, axis=0)
    numerator, colsum, weighted = (numerator, colsum, weighted)
    matched = numerator / colsum[:, None]
    score = (weighted / colsum)[None, :]
    merged = nested_sum(matched.astype(jnp.bfloat16), "client") / lax.axis_size("client")
    return (merged, score)


def solution(mesh):
    in_specs = (
        P(),
        P(("client", "unit"), None),
        P(),
        P("client", None, "unit"),
        P("client", None, "unit"),
        P("client", "unit"),
        P("client", "unit"),
    )
    out_specs = (P("unit", None), P("client", "unit"))
    return jax.shard_map(body, mesh=mesh, in_specs=in_specs, out_specs=out_specs, check_vma=False)
```

profile of v0, /device:TPU:17, one launch (start us, length us, event | category | flops | bytes accessed | tf_op | source)
XLA Modules:
  0.0 313.0 jit_solution(14013043354471950132)
XLA Ops:
  7.2 5.5 %fusion.51 = f32[256,4096]{1,0:T(8,128)} fusion(bf16[512,4096]{1,0:T(8,128)(2,1)} %param.8, s32[512]{0:T(512)S(1)} %iota_add_fusion, s32[256]{0:T(256)} %param.7), kind=kOutput, calls=%fused_computation.49 | convolution fusion | flops 1073872896 | bytes 8391680 | tf_op jit(solution)/shard_map/dot_general | solution.py:84
  12.8 155.3 %all-reduce.2.cloned.1.call-done = f32[256,4096]{1,0:T(8,128)} async-done(((f32[256,4096]{1,0:T(8,128)}), f32[256,4096]{1,0:T(8,128)}) %all-reduce.2.cloned.1.call-update) | async-done | bytes 4194320 | tf_op jit(solution)/shard_map/psum | solution.py:85
  168.1 2.7 multiply_reduce_fusion.3
  170.8 0.7 copy-done.2
  171.6 0.6 multiply_convert_fusion
  172.2 5.7 %fusion.2 = f32[256,896]{1,0:T(8,128)S(1)} fusion(bf16[256,4096]{1,0:T(8,128)(2,1)S(1)} %multiply_convert_fusion, bf16[1,4096,896]{2,1,0:T(8,128)(2,1)} %param.10), kind=kOutput, calls=%fused_computation.2 | convolution fusion | flops 1879048192 | bytes 10354688 | tf_op jit(solution)/shard_map/dot_general | solution.py:89
  177.9 2.4 fusion.69
  180.5 0.9 divide_convert_fusion
  181.4 0.3 fusion.58
  181.7 0.3 fusion.60
  182.0 0.1 pad_maximum_fusion
  182.2 1.8 copy.9
  183.9 33.0 %all_to_all.20 = f32[16,512,56]{1,2,0:T(8,128)S(1)} all-to-all(f32[16,512,56]{1,2,0:T(8,128)} %bitcast.27), channel_id=1, replica_groups=mesh['client'=16,'unit'=8] {'client'}, dimensions={0} | all-to-all | bytes 3670016 | tf_op jit(solution)/shard_map/all_to_all | solution.py:17
  216.9 0.1 reduce_sum.141
  217.1 0.1 fusion.68
  217.2 0.2 multiply_reduce_fusion.6
  217.5 13.4 %all_to_all.21 = bf16[16,256,56]{1,2,0:T(8,128)(2,1)S(1)} all-to-all(bf16[16,256,56]{1,2,0:T(8,128)(2,1)S(1)} %broadcast_in_dim.4), channel_id=1, replica_groups=mesh['client'=16,'unit'=8] {'client'}, dimensions={0} | all-to-all | bytes 917504 | tf_op jit(solution)/shard_map/all_to_all | solution.py:36
  230.9 30.7 %all-gather.2.cloned.1.call-done = bf16[256,7168]{1,0:T(8,128)(2,1)} async-done(((bf16[256,896]{1,0:T(8,128)(2,1)}), bf16[256,7168]{1,0:T(8,128)(2,1)}) %all-gather.2.cloned.1.call-update) | async-done | bytes 3670032 | tf_op jit(solution)/shard_map/all_gather | solution.py:102
  261.6 3.4 %multiply_reduce_fusion.2 = (f32[896]{0:T(1024)S(1)}, f32[896]{0:T(1024)S(1)}, f32[2048,896]{1,0:T(8,128)S(1)}) fusion(bf16[256,896]{0,1:T(8,128)(2,1)S(1)} %bitcast.29, bf16[256,7168]{1,0:T(8,128)(2,1)} %all-gather.2.cloned.1.call-done), kind=kOutput, calls=%fused_computation.6 | convolution fusion | flops 948697344 | bytes 8854528 | tf_op jit(solution)/shard_map/dot_general | solution.py:109
  265.0 2.2 multiply_reduce_fusion.1
  267.2 2.2 multiply_reduce_fusion
  269.4 1.1 multiply_reduce_fusion.4
  270.5 1.2 fusion.10
  271.7 1.2 fusion.33
  272.9 1.2 fusion.30
  274.1 0.8 fusion.39
  274.8 15.8 %all_to_all.22 = bf16[16,56,256]{2,1,0:T(8,128)(2,1)S(1)} all-to-all(bf16[16,56,256]{2,1,0:T(8,128)(2,1)S(1)} %bitcast.33), channel_id=1, replica_groups=mesh['client'=16,'unit'=8] {'client'}, dimensions={0} | all-to-all | bytes 917504 | tf_op jit(solution)/shard_map/all_to_all | solution.py:50
  290.7 0.8 broadcast_in_dim.5
  291.5 4.7 %all-to-all-start.3 = ((bf16[16,56,256]{2,1,0:T(8,128)(2,1)}), bf16[16,56,256]{2,1,0:T(8,128)(2,1)S(1)}, u32[]{:S(2)}, u32[]{:S(2)}) async-start(bf16[16,56,256]{2,1,0:T(8,128)(2,1)} %broadcast_in_dim.5), calls=%async_computation.3 | async-start | bytes 917504 | tf_op jit(solution)/shard_map/all_to_all | solution.py:36
  296.3 0.6 div.89
  296.8 8.4 %all-to-all-done.3 = bf16[16,56,256]{2,1,0:T(8,128)(2,1)S(1)} async-done(((bf16[16,56,256]{2,1,0:T(8,128)(2,1)}), bf16[16,56,256]{2,1,0:T(8,128)(2,1)S(1)}, u32[]{:S(2)}, u32[]{:S(2)}) %all-to-all-start.3) | async-done | bytes 458784 | tf_op jit(solution)/shard_map/all_to_all | solution.py:36
  305.2 1.0 convert_multiply_fusion
  (31 shorter events, 0.5 us)
Async XLA Ops:
  7.2 174.2 %copy-start = (bf16[256,896]{1,0:T(8,128)(2,1)S(1)}, bf16[256,896]{1,0:T(8,128)(2,1)}, u32[]{:S(2)}) copy-start(bf16[256,896]{1,0:T(8,128)(2,1)} %param.13) | copy-start | bytes 1376260
  7.2 160.9 %all-reduce.2.cloned.1.call-start = ((), (), s32[]{:S(2)}) async-start(), calls=%async_computation.4 | async-start | bytes 8388608 | tf_op jit(solution)/shard_map/psum | solution.py:85
  12.8 158.1 %copy-start.5 = (f32[4096]{0:T(1024)S(1)}, f32[4096]{0:T(1024)}, u32[]{:S(2)}) copy-start(f32[4096]{0:T(1024)} %param.9) | copy-start | bytes 49156
  12.8 248.8 %all-gather.2.cloned.1.call-start = ((), (), s32[]{:S(2)}) async-start(), calls=%async_computation.5 | async-start | bytes 4128768 | tf_op jit(solution)/shard_map/all_gather | solution.py:102
  168.1 3.4 %copy-start.2 = (f32[256,4096]{1,0:T(8,128)S(1)}, f32[256,4096]{1,0:T(8,128)}, u32[]{:S(2)}) copy-start(f32[256,4096]{1,0:T(8,128)} %all-reduce.2.cloned.1.call-done) | copy-start | bytes 12582916
  171.6 6.3 %slice-start = ((s8[7340032]{0:T(1024)(128)(4,1)}), s8[3145728]{0:T(1024)(128)(4,1)S(1)}, s32[]{:S(2)}) async-start(s8[7340032]{0:T(1024)(128)(4,1)} %bitcast.34), calls=%async_computation.6 | async-start | bytes 6291456
  172.1 5.7 %slice-start.1 = ((s8[7340032]{0:T(1024)(128)(4,1)}), s8[4194304]{0:T(1024)(128)(4,1)S(1)}, s32[]{:S(2)}) async-start(s8[7340032]{0:T(1024)(128)(4,1)} %bitcast.34), calls=%async_computation.7 | async-start | bytes 8388608
  180.3 1.4 copy-start.4
  261.6 3.4 %copy-start.3 = (bf16[256,7168]{1,0:T(8,128)(2,1)S(1)}, bf16[256,7168]{1,0:T(8,128)(2,1)}, u32[]{:S(2)}) copy-start(bf16[256,7168]{1,0:T(8,128)(2,1)} %all-gather.2.cloned.1.call-done) | copy-start | bytes 11010052
  274.1 32.1 %copy-start.1 = (bf16[256,896]{1,0:T(8,128)(2,1)S(1)}, bf16[256,896]{1,0:T(8,128)(2,1)}, u32[]{:S(2)}) copy-start(bf16[256,896]{1,0:T(8,128)(2,1)} %param.13) | copy-start | bytes 1376260
  291.5 13.7 %all-to-all-start.3 = ((bf16[16,56,256]{2,1,0:T(8,128)(2,1)}), bf16[16,56,256]{2,1,0:T(8,128)(2,1)S(1)}, u32[]{:S(2)}, u32[]{:S(2)}) async-start(bf16[16,56,256]{2,1,0:T(8,128)(2,1)} %broadcast_in_dim.5), calls=%async_computation.3 | async-start | bytes 917504 | tf_op jit(solution)/shard_map/all_to_all | solution.py:36
Sparse Core Ops, SparseCore 0:
  12.9 155.1 all-reduce.1
  181.5 80.0 all-gather.1
where the time goes:
time: 315 us; the launch traced here: 313 us
  waiting for transfers between devices  194 us (62%)
  blocking collectives  62.2 us (20%)
  matrix products  27.4 us (9%)
  between operations  14.3 us (5%)
  other arithmetic  6.02 us (2%)
  starting transfers between devices  4.82 us (2%)
  local copies, waits for them, and re-layouts  3.95 us (1%)
    psum x1, waiting for transfers between devices, body(): embedded = lax.psum(partial_rows, ('client', 'unit'))  155 us
    all_to_all x1, blocking collectives, summed_on_arrival(): blocks = lax.all_to_all(split_up(shard, dim, count), axis, 0, 0, tiled=True)  33 us
    all_gather x1, waiting for transfers between devices, body(): segment = lax.all_gather(client_std, 'unit', axis=1, tiled=True)  30.7 us
    all_to_all x1, blocking collectives, sent_and_summed(): lax.all_to_all(blocks, axis, split_axis=0, concat_axis=0, tiled=True)  15.8 us
    all_to_all x1, blocking collectives, copy_for_each(): return lax.all_to_all(copies, axis, split_axis=0, concat_axis=0, tiled=True)  13.4 us
    dot_general x4, matrix products, body(): jnp.dot(columns.T, ref_std, preferred_element_type=jnp.float32)  8.85 us
    all_to_all x1, waiting for transfers between devices, copy_for_each(): return lax.all_to_all(copies, axis, split_axis=0, concat_axis=0, tiled=True)  8.36 us
  transfers between devices with their start and end apart: 3, of which 3 were waited for; matrix products, arithmetic and copies ran while one was open for 1% of the time, Pallas kernels for 0%

commit v1 on v0

--- a/solution.py
+++ b/solution.py
@@ -1,10 +1,209 @@
 import jax
 import jax.numpy as jnp
 from jax import lax
+from jax.experimental import pallas as pl
+from jax.experimental.pallas import tpu as pltpu
 from jax.sharding import PartitionSpec as P
 
 sharpness = 40.0
 block_cols = 2048
+MESH = pl.DeviceIdType.MESH
+
+TOK = 256
+D = 4096
+HALF = D // 2
+PARTS = ((0, 640), (640, 640), (1280, 768))
+ORDERS = ("xyz", "yzx", "zxy")
+
+
+class Place:
+    def __init__(self):
+        client = lax.axis_index("client")
+        unit = lax.axis_index("unit")
+        self.core = client % 2
+        self.x = (client // 2) % 4
+        self.y = (unit % 2) * 2 + client // 8
+        self.z = unit // 2
+
+    def at(self, axis):
+        return getattr(self, axis)
+
+    def peer(self, axis, step):
+        x, y, z, core = self.x, self.y, self.z, self.core
+        if axis == "x":
+            x = (x + step) % 4
+        elif axis == "y":
+            y = (y + step) % 4
+        elif axis == "z":
+            z = (z + step) % 4
+        else:
+            core = 1 - core
+        return {"client": (y % 2) * 8 + x * 2 + core, "unit": z * 2 + y // 2}
+
+
+def send(src, dst, ssem, rsem, peer):
+    copy = pltpu.make_async_remote_copy(
+        src_ref=src, dst_ref=dst, send_sem=ssem, recv_sem=rsem, device_id=peer, device_id_type=MESH
+    )
+    copy.start()
+    return copy
+
+
+def rows(start, size):
+    return pl.ds(pl.multiple_of(start, size), size)
+
+
+def embed_kernel(ids_ref, gain_ref, table_ref, out_ref, *scratch):
+    tabs = scratch[0:6]
+    accs = scratch[6:9]
+    outs = scratch[9:12]
+    cins = scratch[12:15]
+    r1s = scratch[15:18]
+    a1s = scratch[18:21]
+    r2s = scratch[21:24]
+    a2s = scratch[24:27]
+    r3s = scratch[27:30]
+    fulls = scratch[30:33]
+    tsem, ssem, rsem = scratch[33:36]
+    me = Place()
+    other = 1 - me.core
+
+    loads = []
+    for k in range(6):
+        p = k % 3
+        off, width = PARTS[p]
+        half = other if k < 3 else me.core
+        col = pl.multiple_of(half * HALF + off, 128)
+        load = pltpu.make_async_copy(table_ref.at[:, pl.ds(col, width)], tabs[k], tsem.at[k])
+        load.start()
+        loads.append(load)
+
+    barrier = pltpu.get_barrier_semaphore()
+    peers = [me.peer(axis, step) for axis in "xyz" for step in (1, 2, 3)] + [me.peer("core", 1)]
+    for peer in peers:
+        pl.semaphore_signal(barrier, inc=1, device_id=peer, device_id_type=MESH)
+
+    start = (lax.axis_index("client") * 8 + lax.axis_index("unit")) * 512
+    table_rows = start + lax.broadcasted_iota(jnp.int32, (TOK, 512), 1)
+    pick = jnp.where(ids_ref[...] == table_rows, 1.0, 0.0).astype(jnp.bfloat16)
+    for p in range(3):
+        loads[p].wait()
+        outs[p][...] = jnp.dot(pick, tabs[p][...], preferred_element_type=jnp.float32).astype(jnp.bfloat16)
+        if p == 0:
+            pl.semaphore_wait(barrier, len(peers))
+        loads[p] = send(outs[p], cins[p], ssem.at[p, 0, 0], rsem.at[p, 0, 0], me.peer("core", 1))
+    sent = loads[:3]
+    for p in range(3):
+        loads[3 + p].wait()
+        accs[p][...] = jnp.dot(pick, tabs[3 + p][...], preferred_element_type=jnp.float32).astype(jnp.bfloat16)
+
+    s1 = [[], [], []]
+    for p in range(3):
+        sent[p].wait()
+        accs[p][...] = accs[p][...] + cins[p][...]
+        axis = ORDERS[p][0]
+        for d in (1, 2, 3):
+            to = (me.at(axis) + d) % 4
+            s1[p].append(
+                send(accs[p].at[rows(to * 64, 64)], r1s[p].at[d - 1], ssem.at[p, 1, d - 1], rsem.at[p, 1, d - 1], me.peer(axis, d))
+            )
+    s2 = [[], [], []]
+    for p in range(3):
+        for copy in s1[p]:
+            copy.wait()
+        own = accs[p][rows(me.at(ORDERS[p][0]) * 64, 64), :]
+        a1s[p][...] = (own + r1s[p][0]) + (r1s[p][1] + r1s[p][2])
+        axis = ORDERS[p][1]
+        for d in (1, 2, 3):
+            to = (me.at(axis) + d) % 4
+            s2[p].append(
+                send(a1s[p].at[rows(to * 16, 16)], r2s[p].at[d - 1], ssem.at[p, 2, d - 1], rsem.at[p, 2, d - 1], me.peer(axis, d))
+            )
+    s3 = [[], [], []]
+    for p in range(3):
+        for copy in s2[p]:
+            copy.wait()
+        own = a1s[p][rows(me.at(ORDERS[p][1]) * 16, 16), :]
+        a2s[p][...] = (own + r2s[p][0]) + (r2s[p][1] + r2s[p][2])
+        axis = ORDERS[p][2]
+        for d in (1, 2, 3):
+            s3[p].append(
+                send(a2s[p], r3s[p].at[d - 1], ssem.at[p, 3, d - 1], rsem.at[p, 3, d - 1], me.peer(axis, d))
+            )
+    s4 = [[], [], []]
+    for p in range(3):
+        for copy in s3[p]:
+            copy.wait()
+        base = me.at(ORDERS[p][0]) * 64 + me.at(ORDERS[p][1]) * 16
+        piece = fulls[p].at[me.core, rows(base, 16)]
+        piece[...] = (a2s[p][...] + r3s[p][0]) + (r3s[p][1] + r3s[p][2])
+        axis = ORDERS[p][1]
+        for d in (1, 2, 3):
+            s4[p].append(send(piece, piece, ssem.at[p, 4, d - 1], rsem.at[p, 4, d - 1], me.peer(axis, d)))
+    s5 = [[], [], []]
+    s6 = [[], [], []]
+    for p in range(3):
+        for copy in s4[p]:
+            copy.wait()
+        axis = ORDERS[p][0]
+        piece = fulls[p].at[me.core, rows(me.at(axis) * 64, 64)]
+        for d in (1, 2, 3):
+            s5[p].append(send(piece, piece, ssem.at[p, 5, d - 1], rsem.at[p, 5, d - 1], me.peer(axis, d)))
+        s6[p].append(send(piece, piece, ssem.at[p, 6, 0], rsem.at[p, 6, 0], me.peer("core", 1)))
+    for p in range(3):
+        axis = ORDERS[p][0]
+        for d in (1, 2, 3):
+            s5[p][d - 1].wait()
+            came = (me.at(axis) + 4 - d) % 4
+            piece = fulls[p].at[me.core, rows(came * 64, 64)]
+            s6[p].append(send(piece, piece, ssem.at[p, 6, d], rsem.at[p, 6, d], me.peer("core", 1)))
+    for p in range(3):
+        for copy in s6[p]:
+            copy.wait()
+
+    for t in range(0, TOK, 32):
+        total = jnp.zeros((32, 1), jnp.float32)
+        for p in range(3):
+            for h in range(2):
+                v = fulls[p][h, pl.ds(t, 32), :].astype(jnp.float32)
+                total = total + jnp.sum(v * v, axis=1, keepdims=True)
+        scale = lax.rsqrt(total * (1.0 / D) + 1e-05)
+        for p, (off, width) in enumerate(PARTS):
+            for h in range(2):
+                v = fulls[p][h, pl.ds(t, 32), :].astype(jnp.float32)
+                cols = pl.ds(h * HALF + off, width)
+                out_ref[pl.ds(t, 32), cols] = (v * scale * gain_ref[:, cols]).astype(jnp.bfloat16)
+
+
+def embed_norm(token_ids, norm_gain, embed_table):
+    bf = jnp.bfloat16
+    widths = [w for _, w in PARTS]
+    shapes = [pltpu.VMEM((512, w), bf) for w in widths * 2]
+    shapes += [pltpu.VMEM((TOK, w), bf) for w in widths * 3]
+    shapes += [pltpu.VMEM((3, 64, w), bf) for w in widths]
+    shapes += [pltpu.VMEM((64, w), bf) for w in widths]
+    shapes += [pltpu.VMEM((3, 16, w), bf) for w in widths]
+    shapes += [pltpu.VMEM((16, w), bf) for w in widths]
+    shapes += [pltpu.VMEM((3, 16, w), bf) for w in widths]
+    shapes += [pltpu.VMEM((2, TOK, w), bf) for w in widths]
+    shapes += [
+        pltpu.SemaphoreType.DMA((6,)),
+        pltpu.SemaphoreType.DMA((3, 7, 4)),
+        pltpu.SemaphoreType.DMA((3, 7, 4)),
+    ]
+    return pl.pallas_call(
+        embed_kernel,
+        out_shape=jax.ShapeDtypeStruct((TOK, D), bf),
+        in_specs=[
+            pl.BlockSpec(memory_space=pltpu.VMEM),
+            pl.BlockSpec(memory_space=pltpu.VMEM),
+            pl.BlockSpec(memory_space=pl.ANY),
+        ],
+        out_specs=pl.BlockSpec(memory_space=pltpu.VMEM),
+        scratch_shapes=shapes,
+        compiler_params=pltpu.CompilerParams(collective_id=0, has_side_effects=True, vmem_limit_bytes=40 << 20),
+        name="embed_norm",
+    )(token_ids[:, None], norm_gain[None, :], embed_table)
 
 
 def split_up(shard, dim, count):
@@ -69,21 +268,8 @@
     return [(offset, min(block_cols, length - offset)) for offset in range(0, length, block_cols)]
 
 
-def rms_scaled(values, norm_gain):
-    scale = lax.rsqrt(jnp.mean(values * values, axis=1, keepdims=True) + 1e-05)
-    return (values * scale * norm_gain[None, :]).astype(jnp.bfloat16)
-
-
 def body(token_ids, embed_table, norm_gain, client_gate, client_up, ref_gate, ref_up):
-    rows_here = embed_table.shape[0]
-    table_start = (
-        lax.axis_index("client") * lax.axis_size("unit") + lax.axis_index("unit")
-    ) * rows_here
-    table_rows = table_start + jnp.arange(rows_here, dtype=jnp.int32)
-    selector = (token_ids[:, None] == table_rows[None, :]).astype(jnp.bfloat16)
-    partial_rows = jnp.dot(selector, embed_table, preferred_element_type=jnp.float32)
-    embedded = lax.psum(partial_rows, ("client", "unit"))
-    normed = rms_scaled(embedded, norm_gain)
+    normed = embed_norm(token_ids, norm_gain, embed_table)
     token_count = normed.shape[0]
     inverse_tokens = 1.0 / token_count
     gate_local = jnp.dot(normed, client_gate[0], preferred_element_type=jnp.float32)

time: 315 us -> 189 us (0.60)
  waiting for transfers between devices: 194 us -> 39.9 us
  Pallas kernels: 0 us -> 36.3 us
  matrix products: 27.4 us -> 21.7 us
  other arithmetic: 6.02 us -> 2.74 us
    psum x1 -> x0, waiting for transfers between devices: 155 us -> none  [body(): embedded = lax.psum(partial_rows, ('client', 'unit'))]
    pallas_call x0 -> x1, Pallas kernels: none -> 36.3 us  [embed_norm(): pl.pallas_call(embed_kernel, out_shape=jax.ShapeDtypeStruct((TOK, D), bf)...]
    dot_general x1 -> x0, matrix products: 5.52 us -> none  [body(): jnp.dot(selector, embed_table, preferred_element_type=jnp.float32)]
  transfers between devices with their start and end apart: 3 -> 2, of which waited for: 3 -> 2; matrix products, arithmetic and copies ran while one was open for 1% -> 2% of each run, Pallas kernels for 0% -> 0%
where the time goes in v1:
time: 189 us; the launch traced here: 187 us
  blocking collectives  60.1 us (32%)
  waiting for transfers between devices  39.9 us (21%)
  Pallas kernels  36.3 us (19%)
  matrix products  21.7 us (11%)
  between operations  14.3 us (8%)
  local copies, waits for them, and re-layouts  6.97 us (4%)
  starting transfers between devices  4.78 us (3%)
  other arithmetic  2.74 us (1%)
    pallas_call x1, Pallas kernels, embed_norm(): pl.pallas_call(embed_kernel, out_shape=jax.ShapeDtypeStruct((TOK, D), bf)...  36.3 us
    all_gather x1, waiting for transfers between devices, body(): segment = lax.all_gather(client_std, 'unit', axis=1, tiled=True)  31.5 us
    all_to_all x1, blocking collectives, summed_on_arrival(): blocks = lax.all_to_all(split_up(shard, dim, count), axis, 0, 0, tiled=True)  30 us
    all_to_all x1, blocking collectives, sent_and_summed(): lax.all_to_all(blocks, axis, split_axis=0, concat_axis=0, tiled=True)  15.8 us
    all_to_all x1, blocking collectives, copy_for_each(): return lax.all_to_all(copies, axis, split_axis=0, concat_axis=0, tiled=True)  14.3 us
    dot_general x4, matrix products, body(): jnp.dot(columns.T, ref_std, preferred_element_type=jnp.float32)  8.85 us
    all_to_all x1, waiting for transfers between devices, copy_for_each(): return lax.all_to_all(copies, axis, split_axis=0, concat_axis=0, tiled=True)  8.36 us
    dot_general x1, matrix products, body(): jnp.dot(normed, client_gate[0], preferred_element_type=jnp.float32)  5.57 us
  transfers between devices with their start and end apart: 2, of which 2 were waited for; matrix products, arithmetic and copies ran while one was open for 2% of the time, Pallas kernels for 0%

profile of v1, /device:TPU:17, one launch (start us, length us, event | category | flops | bytes accessed | tf_op | source)
XLA Modules:
  0.0 186.7 jit_solution(6042848738385841892)
XLA Ops:
  7.2 0.9 copy.9.ids_ref
  8.1 2.2 %copy-done.2 = bf16[512,4096]{1,0:T(8,128)(2,1)S(1)} copy-done((bf16[512,4096]{1,0:T(8,128)(2,1)S(1)}, bf16[512,4096]{1,0:T(8,128)(2,1)}, u32[]{:S(2)}) %copy-start.2) | copy-done | bytes 4194328
  10.3 0.7 copy-done.3
  11.0 36.3 %embed_norm.1 = bf16[256,4096]{1,0:T(8,128)(2,1)S(1)} custom-call(s32[256,1]{1,0:T(8,128)S(1)} %copy.9.ids_ref, f32[1,4096]{1,0:T(1,128)S(1)} %bitcast.28, bf16[512,4096]{1,0:T(8,128)(2,1)S(1)} %copy-done.2), custom_call_target="tpu_custom_call" | custom-call | tf_op jit(solution)/shard_map/embed_norm/pallas_call | solution.py:194
  47.3 5.6 %fusion.2 = f32[256,896]{1,0:T(8,128)S(1)} fusion(bf16[256,4096]{1,0:T(8,128)(2,1)S(1)} %embed_norm.1, bf16[1,4096,896]{2,1,0:T(8,128)(2,1)} %param.10), kind=kOutput, calls=%fused_computation.2 | convolution fusion | flops 1879048192 | bytes 10354688 | tf_op jit(solution)/shard_map/dot_general | solution.py:275
  52.9 2.4 %fusion.65 = (f32[896]{0:T(1024)S(1)}, f32[256,896]{1,0:T(8,128)S(1)}) fusion(bf16[256,4096]{1,0:T(8,128)(2,1)S(1)} %embed_norm.1, bf16[1,4096,896]{2,1,0:T(8,128)(2,1)S(1)} %bitcast.38, f32[256,896]{1,0:T(8,128)S(1)} %fusion.2), kind=kOutput, calls=%fused_computation.70 | convolution fusion | flops 1880423552 | bytes 11275776 | tf_op jit(solution)/shard_map/dot_general | solution.py:276
  55.3 0.1 multiply_reduce_fusion.4
  55.4 0.9 divide_convert_fusion
  56.3 0.3 fusion.54
  56.6 0.3 fusion.56
  56.9 0.1 pad_maximum_fusion
  57.1 1.8 copy.10
  58.8 30.0 %all_to_all.20 = f32[16,512,56]{1,2,0:T(8,128)S(1)} all-to-all(f32[16,512,56]{1,2,0:T(8,128)} %bitcast.29), channel_id=1, replica_groups=mesh['client'=16,'unit'=8] {'client'}, dimensions={0} | all-to-all | bytes 3670016 | tf_op jit(solution)/shard_map/all_to_all | solution.py:216
  88.8 0.1 reduce_sum.131
  88.9 0.1 fusion.64
  89.1 0.2 multiply_reduce_fusion.5
  89.4 14.3 %all_to_all.21 = bf16[16,256,56]{1,2,0:T(8,128)(2,1)S(1)} all-to-all(bf16[16,256,56]{1,2,0:T(8,128)(2,1)S(1)} %broadcast_in_dim.20), channel_id=1, replica_groups=mesh['client'=16,'unit'=8] {'client'}, dimensions={0} | all-to-all | bytes 917504 | tf_op jit(solution)/shard_map/all_to_all | solution.py:235
  103.7 31.5 %all-gather.2.cloned.1.call-done = bf16[256,7168]{1,0:T(8,128)(2,1)} async-done(((bf16[256,896]{1,0:T(8,128)(2,1)}), bf16[256,7168]{1,0:T(8,128)(2,1)}) %all-gather.2.cloned.1.call-update) | async-done | bytes 3670032 | tf_op jit(solution)/shard_map/all_gather | solution.py:288
  135.3 3.4 %multiply_reduce_fusion.2 = (f32[896]{0:T(1024)S(1)}, f32[896]{0:T(1024)S(1)}, f32[2048,896]{1,0:T(8,128)S(1)}) fusion(bf16[256,896]{0,1:T(8,128)(2,1)S(1)} %bitcast.31, bf16[256,7168]{1,0:T(8,128)(2,1)} %all-gather.2.cloned.1.call-done), kind=kOutput, calls=%fused_computation.6 | convolution fusion | flops 948697344 | bytes 8854528 | tf_op jit(solution)/shard_map/dot_general | solution.py:295
  138.7 2.2 %multiply_reduce_fusion.1 = (f32[896]{0:T(1024)S(1)}, f32[896]{0:T(1024)S(1)}, f32[2048,896]{1,0:T(8,128)S(1)}) fusion(bf16[256,896]{0,1:T(8,128)(2,1)S(1)} %bitcast.32, bf16[256,7168]{1,0:T(8,128)(2,1)S(1)} %copy-done.4), kind=kOutput, calls=%fused_computation.5 | convolution fusion | flops 948697344 | bytes 8854528 | tf_op jit(solution)/shard_map/dot_general | solution.py:295
  140.9 2.2 %multiply_reduce_fusion = (f32[896]{0:T(1024)S(1)}, f32[896]{0:T(1024)S(1)}, f32[2048,896]{1,0:T(8,128)S(1)}) fusion(bf16[256,896]{0,1:T(8,128)(2,1)S(1)} %bitcast.33, bf16[256,7168]{1,0:T(8,128)(2,1)S(1)} %copy-done.4), kind=kOutput, calls=%fused_computation.4 | convolution fusion | flops 948697344 | bytes 8854528 | tf_op jit(solution)/shard_map/dot_general | solution.py:295
  143.0 1.1 multiply_reduce_fusion.3
  144.2 1.2 fusion.10
  145.3 1.2 fusion.33
  146.5 1.2 fusion.30
  147.7 0.8 fusion.39
  148.5 15.8 %all_to_all.22 = bf16[16,56,256]{2,1,0:T(8,128)(2,1)S(1)} all-to-all(bf16[16,56,256]{2,1,0:T(8,128)(2,1)S(1)} %bitcast.35), channel_id=1, replica_groups=mesh['client'=16,'unit'=8] {'client'}, dimensions={0} | all-to-all | bytes 917504 | tf_op jit(solution)/shard_map/all_to_all | solution.py:249
  164.4 0.8 broadcast_in_dim.21
  165.2 4.7 %all-to-all-start.3 = ((bf16[16,56,256]{2,1,0:T(8,128)(2,1)}), bf16[16,56,256]{2,1,0:T(8,128)(2,1)S(1)}, u32[]{:S(2)}, u32[]{:S(2)}) async-start(bf16[16,56,256]{2,1,0:T(8,128)(2,1)} %broadcast_in_dim.21), calls=%async_computation.3 | async-start | bytes 917504 | tf_op jit(solution)/shard_map/all_to_all | solution.py:235
  169.9 0.6 div.81
  170.5 8.4 %all-to-all-done.3 = bf16[16,56,256]{2,1,0:T(8,128)(2,1)S(1)} async-done(((bf16[16,56,256]{2,1,0:T(8,128)(2,1)}), bf16[16,56,256]{2,1,0:T(8,128)(2,1)S(1)}, u32[]{:S(2)}, u32[]{:S(2)}) %all-to-all-start.3) | async-done | bytes 458784 | tf_op jit(solution)/shard_map/all_to_all | solution.py:235
  178.9 1.0 convert_multiply_fusion
  (25 shorter events, 0.3 us)
Async XLA Ops:
  7.2 49.1 %copy-start = (bf16[256,896]{1,0:T(8,128)(2,1)S(1)}, bf16[256,896]{1,0:T(8,128)(2,1)}, u32[]{:S(2)}) copy-start(bf16[256,896]{1,0:T(8,128)(2,1)} %param.13) | copy-start | bytes 1376260
  7.2 128.1 %all-gather.2.cloned.1.call-start = ((), (), s32[]{:S(2)}) async-start(), calls=%async_computation.4 | async-start | bytes 4128768 | tf_op jit(solution)/shard_map/all_gather | solution.py:288
  8.1 2.2 %copy-start.2 = (bf16[512,4096]{1,0:T(8,128)(2,1)S(1)}, bf16[512,4096]{1,0:T(8,128)(2,1)}, u32[]{:S(2)}) copy-start(bf16[512,4096]{1,0:T(8,128)(2,1)} %table_ref.1) | copy-start | bytes 12582916
  10.3 0.7 copy-start.3
  11.0 41.9 %slice-start = ((s8[7340032]{0:T(1024)(128)(4,1)}), s8[3145728]{0:T(1024)(128)(4,1)S(1)}, s32[]{:S(2)}) async-start(s8[7340032]{0:T(1024)(128)(4,1)} %bitcast.37), calls=%async_computation.5 | async-start | bytes 6291456
  47.3 5.6 %slice-start.1 = ((s8[7340032]{0:T(1024)(128)(4,1)}), s8[4194304]{0:T(1024)(128)(4,1)S(1)}, s32[]{:S(2)}) async-start(s8[7340032]{0:T(1024)(128)(4,1)} %bitcast.37), calls=%async_computation.6 | async-start | bytes 8388608
  55.3 1.4 copy-start.5
  135.3 3.4 %copy-start.4 = (bf16[256,7168]{1,0:T(8,128)(2,1)S(1)}, bf16[256,7168]{1,0:T(8,128)(2,1)}, u32[]{:S(2)}) copy-start(bf16[256,7168]{1,0:T(8,128)(2,1)} %all-gather.2.cloned.1.call-done) | copy-start | bytes 11010052
  147.7 32.1 %copy-start.1 = (bf16[256,896]{1,0:T(8,128)(2,1)S(1)}, bf16[256,896]{1,0:T(8,128)(2,1)}, u32[]{:S(2)}) copy-start(bf16[256,896]{1,0:T(8,128)(2,1)} %param.13) | copy-start | bytes 1376260
  165.2 13.7 %all-to-all-start.3 = ((bf16[16,56,256]{2,1,0:T(8,128)(2,1)}), bf16[16,56,256]{2,1,0:T(8,128)(2,1)S(1)}, u32[]{:S(2)}, u32[]{:S(2)}) async-start(bf16[16,56,256]{2,1,0:T(8,128)(2,1)} %broadcast_in_dim.21), calls=%async_computation.3 | async-start | bytes 917504 | tf_op jit(solution)/shard_map/all_to_all | solution.py:235
Sparse Core Ops, SparseCore 0:
  56.4 78.7 all-gather.1

commit v2 on v1

--- a/solution.py
+++ b/solution.py
@@ -6,7 +6,6 @@
 from jax.sharding import PartitionSpec as P
 
 sharpness = 40.0
-block_cols = 2048
 MESH = pl.DeviceIdType.MESH
 
 TOK = 256
@@ -39,6 +38,16 @@
         else:
             core = 1 - core
         return {"client": (y % 2) * 8 + x * 2 + core, "unit": z * 2 + y // 2}
+
+
+    def plane_peer(self, dx, flip, hflip):
+        x = (self.x + dx) % 4
+        low = (self.y % 2 + flip) % 2
+        high = (self.y // 2 + hflip) % 2
+        return {"client": low * 8 + x * 2 + self.core, "unit": self.z * 2 + high}
+
+    def plane_piece(self, dx, flip):
+        return ((self.x + dx) % 4) * 2 + (self.y % 2 + flip) % 2
 
 
 def send(src, dst, ssem, rsem, peer):
@@ -205,109 +214,288 @@
         name="embed_norm",
     )(token_ids[:, None], norm_gain[None, :], embed_table)
 
-
-def split_up(shard, dim, count):
-    before, after = (shard.shape[:dim], shard.shape[dim + 1 :])
-    return jnp.moveaxis(shard.reshape(*before, count, -1, *after), dim, 0)
-
-
-def summed_on_arrival(shard, axis, dim):
-    count = lax.axis_size(axis)
-    blocks = lax.all_to_all(split_up(shard, dim, count), axis, 0, 0, tiled=True)
-    return jnp.sum(blocks, axis=0)
-
-
-def sent_together(arrays, axis, dim, along):
-    widths = [a.shape[along] for a in arrays]
-    both = jnp.concatenate(arrays, axis=along)
-    result = summed_on_arrival(both, axis, dim)
-    return tuple(jnp.split(result, [sum(widths[:k]) for k in range(1, len(widths))], axis=along))
-
-
-def laid_out(blocks, dim):
-    dims = list(blocks.shape[1:])
-    dims[dim] *= blocks.shape[0]
-    return jnp.moveaxis(blocks, 0, dim).reshape(dims)
-
-
-def copy_for_each(shard, axis):
-    copies = jnp.broadcast_to(shard, (lax.axis_size(axis), *shard.shape))
-    return lax.all_to_all(copies, axis, split_axis=0, concat_axis=0, tiled=True)
-
-
-def gather_directly(shard, axis, dim):
-    return laid_out(copy_for_each(shard, axis), dim)
-
-
-def filled_up(lines, count):
-    spare = -len(lines) % count
-    return jnp.pad(lines, [(0, spare)] + [(0, 0)] * (lines.ndim - 1))
-
-
-def sent_and_summed(shard, axis, dim):
-    blocks = split_up(shard, dim, lax.axis_size(axis))
-    arrived = lax.all_to_all(blocks, axis, split_axis=0, concat_axis=0, tiled=True)
-    return arrived.astype(jnp.float32).sum(axis=0)
-
-
-def nested_sum(shard, axes):
-    lines = shard.reshape(-1, shard.shape[-1])
-    padded = filled_up(lines, lax.axis_size(axes))
-    whole = gather_directly(sent_and_summed(padded, axes, 0).astype(jnp.bfloat16), axes, 0)
-    return lax.slice_in_dim(whole, 0, len(lines)).reshape(shard.shape).astype(jnp.float32)
-
-
-def standardize(hidden):
-    center = jnp.mean(hidden, axis=0, keepdims=True)
-    shifted = hidden - center
-    spread = jnp.sqrt(jnp.mean(shifted * shifted, axis=0, keepdims=True) + 1e-06)
-    return (shifted / spread).astype(jnp.bfloat16)
-
-
-def block_ranges(length):
-    return [(offset, min(block_cols, length - offset)) for offset in range(0, length, block_cols)]
+FF_HERE = 896
+PIECE = 112
+JOINT = 2 * FF_HERE
+JC = 224
+SPANS = ((0, 256), (256, 256), (512, 256), (768, 128))
+RING8 = [(dx, f) for dx in range(4) for f in range(2)][1:]
+RING16 = [(dx, f, h) for h in range(2) for dx in range(4) for f in range(2)][1:]
+EXP_SCALE = sharpness / TOK * 1.4426950408889634
+
+
+def spread(h, axis):
+    center = jnp.mean(h, axis=axis, keepdims=True)
+    shifted = h - center
+    width = jnp.sqrt(jnp.mean(shifted * shifted, axis=axis, keepdims=True) + 1e-06)
+    return (shifted / width).astype(jnp.bfloat16)
+
+
+def gated(g, u):
+    return g / (1.0 + jnp.exp(-g)) * u
+
+
+def align_kernel(
+    x_ref, cg_ref, cu_ref, rg_ref, ru_ref, merged_ref, score_ref,
+    w, rw, part, pin, tb, r2, swap, swin, refs, units, wts, num, cs, ws, col, colin,
+    nout, nin, nsum, f2, fin, wsem, rwsem, csem, crsem, zs, zr, xs, xr,
+):
+    me = Place()
+    core, other = me.core, 1 - me.core
+    mate = me.peer("core", 1)
+
+    refload = []
+    for k, src in enumerate((rg_ref, ru_ref)):
+        load = pltpu.make_async_copy(src, rw.at[k], rwsem.at[k])
+        load.start()
+        refload.append(load)
+    wload = {}
+    for q in range(3):
+        for k, src in enumerate((cg_ref, cu_ref)):
+            load = pltpu.make_async_copy(
+                src.at[0, :, pl.ds(q * 256, 256)], w.at[q * 2 + k], wsem.at[q * 2 + k]
+            )
+            load.start()
+            wload[q, k] = load
+    for k, src in enumerate((cg_ref, cu_ref)):
+        load = pltpu.make_async_copy(
+            src.at[0, :, pl.ds(768, 128)], w.at[6, :, pl.ds(k * 128, 128)], wsem.at[6 + k]
+        )
+        load.start()
+        wload[3, k] = load
+
+    barrier = pltpu.get_barrier_semaphore()
+    peers = [me.plane_peer(*r) for r in RING16] + [me.peer("z", 1), me.peer("z", 3), mate]
+    for peer in peers:
+        pl.semaphore_signal(barrier, inc=1, device_id=peer, device_id_type=MESH)
+
+    span = pl.ds(pl.multiple_of(lax.axis_index("client") * 256, 256), 256)
+    xpart = x_ref[:, span]
+    for k in range(2):
+        refload[k].wait()
+        part[k] = jnp.dot(xpart, rw[k], preferred_element_type=jnp.float32).T
+    pl.semaphore_wait(barrier, len(peers))
+    c1 = send(part.at[other], pin, csem.at[0], crsem.at[0], mate)
+
+    zcopies = []
+
+    def client_block(q):
+        start, width = SPANS[q]
+        for k in range(2):
+            wload[q, k].wait()
+        if q < 3:
+            g = jnp.dot(x_ref[...], w[q * 2], preferred_element_type=jnp.float32)
+            u = jnp.dot(x_ref[...], w[q * 2 + 1], preferred_element_type=jnp.float32)
+        else:
+            both = jnp.dot(x_ref[...], w[6], preferred_element_type=jnp.float32)
+            g, u = both[:, :128], both[:, 128:]
+        cols = pl.ds(start, width)
+        units[0, :, cols] = spread(gated(g, u), 0)
+        mine = units.at[0, :, cols]
+        zcopies.append((
+            send(mine, units.at[1, :, cols], zs.at[0, q], zr.at[0, q], me.peer("z", 1)),
+            send(mine, units.at[3, :, cols], zs.at[1, q], zr.at[1, q], me.peer("z", 3)),
+        ))
+
+    relays = []
+
+    def relay(q):
+        cols = pl.ds(*SPANS[q])
+        if q in (0, 3):
+            zcopies[q][0].wait_recv()
+            relays.append(send(units.at[1, :, cols], units.at[2, :, cols], zs.at[2, q], zr.at[2, q], me.peer("z", 1)))
+        else:
+            zcopies[q][1].wait_recv()
+            relays.append(send(units.at[3, :, cols], units.at[2, :, cols], zs.at[2, q], zr.at[2, q], me.peer("z", 3)))
+
+    client_block(0)
+    c1.wait()
+    tb[...] = (part[core] + pin[...]).astype(jnp.bfloat16)
+    c2 = []
+    for n, (dx, f) in enumerate(RING8):
+        rows_to = rows(me.plane_piece(dx, f) * PIECE, PIECE)
+        c2.append(send(tb.at[rows_to], r2.at[n], xs.at[0, n], xr.at[0, n], me.plane_peer(dx, f, 0)))
+    client_block(1)
+    client_block(2)
+    client_block(3)
+    here = me.plane_piece(0, 0)
+    total = tb[rows(here * PIECE, PIECE), :].astype(jnp.float32)
+    for n in range(7):
+        c2[n].wait()
+        total = total + r2[n].astype(jnp.float32)
+    swap[...] = total
+    c3 = send(swap, swin, csem.at[1], crsem.at[1], mate)
+    relay(0)
+    c3.wait()
+    mine = swap[...]
+    theirs = swin[...]
+    first = core == 0
+    g = jnp.where(first, mine, theirs)
+    u = jnp.where(first, theirs, mine)
+    piece_rows = rows((me.y // 2) * FF_HERE + here * PIECE, PIECE)
+    half = pl.ds(pl.multiple_of(core * 128, 128), 128)
+    piece_std = spread(gated(g, u), 1)
+    refs[piece_rows, half] = jnp.where(first, piece_std[:, :128], piece_std[:, 128:])
+    c4 = []
+    for n, (dx, f, h) in enumerate(RING16):
+        piece = refs.at[piece_rows, half]
+        c4.append(send(piece, piece, xs.at[1, n], xr.at[1, n], me.plane_peer(dx, f, h)))
+    relay(1)
+    for copy in c4:
+        copy.wait()
+    c5 = send(refs.at[:, half], refs.at[:, half], csem.at[2], crsem.at[2], mate)
+    relay(2)
+    c5.wait()
+
+    def align(slot, first, block):
+        @pl.loop(0, FF_HERE // JC)
+        def _(t):
+            js = rows(block * FF_HERE + t * JC, JC)
+            r = refs[js, :]
+            a = jnp.zeros((JC, 128), jnp.float32) if first else cs[js, :]
+            b = jnp.zeros((JC, 128), jnp.float32) if first else ws[js, :]
+            for start, width in SPANS:
+                s = jnp.dot(r, units[slot, :, pl.ds(start, width)], preferred_element_type=jnp.float32)
+                e = jnp.exp2(s * EXP_SCALE)
+                wts[:, pl.ds(start, width)] = e.astype(jnp.bfloat16)
+                es = e * s
+                for o in range(0, width, 128):
+                    a = a + e[:, o : o + 128]
+                    b = b + es[:, o : o + 128]
+            cs[js, :] = a
+            ws[js, :] = b
+            got = lax.dot_general(
+                wts[...], units[slot], (((1,), (1,)), ((), ())), preferred_element_type=jnp.float32
+            )
+            num[js, :] = got if first else num[js, :] + got
+
+    align(0, True, 0)
+    align(0, True, 1)
+    relay(3)
+    for slot, way, forwarded in ((1, 0, (0, 3)), (3, 1, (1, 2))):
+        for q in range(4):
+            if q not in forwarded:
+                zcopies[q][way].wait_recv()
+        for block in range(2):
+            align(slot, False, block)
+    for copy in relays:
+        copy.wait_recv()
+
+    eye = lax.broadcasted_iota(jnp.int32, (128, 128), 0) == lax.broadcasted_iota(jnp.int32, (128, 128), 1)
+
+    def to_row(v):
+        return jnp.sum(jnp.where(eye, jnp.sum(v, axis=1, keepdims=True), 0.0), axis=0, keepdims=True)
+
+    c6 = []
+    for block in range(2):
+        align(2, False, block)
+        for q in range(7):
+            js = pl.ds(block * FF_HERE + q * 128, 128)
+            col[block, pl.ds(q, 1), :] = to_row(cs[js, :])
+            col[block, pl.ds(q + 8, 1), :] = to_row(ws[js, :])
+        c6.append(send(col.at[block], colin.at[block], csem.at[3 + block], crsem.at[3 + block], me.peer("y", 2)))
+
+    c7 = []
+    for block in range(2):
+        c6[block].wait()
+        for q in range(7):
+            js = pl.ds(block * FF_HERE + q * 128, 128)
+            inv = 1.0 / (col[block, pl.ds(q, 1), :] + colin[block, pl.ds(q, 1), :])
+            inv = jnp.sum(jnp.where(eye, inv, 0.0), axis=1, keepdims=True)
+            n = (num[js, :] * inv).astype(jnp.bfloat16)
+            nout[0, js, :] = n[:, :128]
+            nout[1, js, :] = n[:, 128:]
+        bs = pl.ds(block * FF_HERE, FF_HERE)
+        c7.append(send(nout.at[other, bs], nin.at[bs], csem.at[5 + block], crsem.at[5 + block], mate))
+
+    mineblock = me.y // 2
+    for q in range(7):
+        below = col[mineblock, pl.ds(q, 1), :] + colin[mineblock, pl.ds(q, 1), :]
+        above = col[mineblock, pl.ds(q + 8, 1), :] + colin[mineblock, pl.ds(q + 8, 1), :]
+        score_ref[:, pl.ds(q * 128, 128)] = above / below * (1.0 / TOK)
+
+    for block in range(2):
+        c7[block].wait()
+        bs = pl.ds(block * FF_HERE, FF_HERE)
+        nsum[bs, :] = nout[core, bs, :] + nin[bs, :]
+    c8 = []
+    for n, (dx, f, h) in enumerate(RING16):
+        to = ((me.y // 2 + h) % 2) * FF_HERE + me.plane_piece(dx, f) * PIECE
+        c8.append(send(nsum.at[rows(to, PIECE)], f2.at[n], xs.at[2, n], xr.at[2, n], me.plane_peer(dx, f, h)))
+    total = nsum[piece_rows, :].astype(jnp.float32)
+    for n in range(15):
+        c8[n].wait()
+        total = total + f2[n].astype(jnp.float32)
+    mine = fin.at[core, here]
+    mine[...] = total.astype(jnp.bfloat16)
+    c9 = []
+    c10 = [send(mine, mine, csem.at[7], crsem.at[7], mate)]
+    for n, (dx, f) in enumerate(RING8):
+        c9.append(send(mine, mine, xs.at[3, n], xr.at[3, n], me.plane_peer(dx, f, 0)))
+    for n, (dx, f) in enumerate(RING8):
+        c9[n].wait()
+        came = fin.at[core, me.plane_piece(4 - dx, f)]
+        c10.append(send(came, came, csem.at[8 + n], crsem.at[8 + n], mate))
+    for copy in c10:
+        copy.wait()
+    for s in range(8):
+        for h in range(2):
+            merged_ref[pl.ds(s * PIECE, PIECE), pl.ds(h * 128, 128)] = fin[h, s].astype(jnp.float32) * (1.0 / 16)
+
+    for pair in zcopies:
+        pair[0].wait_send()
+        pair[1].wait_send()
+    for copy in relays:
+        copy.wait_send()
+
+
+def aligned(normed, client_gate, client_up, ref_gate, ref_up):
+    bf, f32 = jnp.bfloat16, jnp.float32
+    dma = pltpu.SemaphoreType.DMA
+    shapes = [
+        pltpu.VMEM((7, D, 256), bf),
+        pltpu.VMEM((2, 256, FF_HERE), bf),
+        pltpu.VMEM((2, FF_HERE, TOK), f32),
+        pltpu.VMEM((FF_HERE, TOK), f32),
+        pltpu.VMEM((FF_HERE, TOK), bf),
+        pltpu.VMEM((7, PIECE, TOK), bf),
+        pltpu.VMEM((PIECE, TOK), f32),
+        pltpu.VMEM((PIECE, TOK), f32),
+        pltpu.VMEM((JOINT, TOK), bf),
+        pltpu.VMEM((4, TOK, FF_HERE), bf),
+        pltpu.VMEM((JC, FF_HERE), bf),
+        pltpu.VMEM((JOINT, TOK), f32),
+        pltpu.VMEM((JOINT, 128), f32),
+        pltpu.VMEM((JOINT, 128), f32),
+        pltpu.VMEM((2, 16, 128), f32),
+        pltpu.VMEM((2, 16, 128), f32),
+        pltpu.VMEM((2, JOINT, 128), bf),
+        pltpu.VMEM((JOINT, 128), bf),
+        pltpu.VMEM((JOINT, 128), bf),
+        pltpu.VMEM((15, PIECE, 128), bf),
+        pltpu.VMEM((2, 8, PIECE, 128), bf),
+        dma((8,)), dma((2,)), dma((15,)), dma((15,)),
+        dma((3, 4)), dma((3, 4)), dma((4, 15)), dma((4, 15)),
+    ]
+    vmem = pl.BlockSpec(memory_space=pltpu.VMEM)
+    hbm = pl.BlockSpec(memory_space=pl.ANY)
+    return pl.pallas_call(
+        align_kernel,
+        out_shape=(
+            jax.ShapeDtypeStruct((FF_HERE, TOK), f32),
+            jax.ShapeDtypeStruct((1, FF_HERE), f32),
+        ),
+        in_specs=[vmem, hbm, hbm, hbm, hbm],
+        out_specs=(vmem, vmem),
+        scratch_shapes=shapes,
+        compiler_params=pltpu.CompilerParams(collective_id=1, has_side_effects=True, vmem_limit_bytes=56 << 20),
+        name="align",
+    )(normed, client_gate, client_up, ref_gate, ref_up)
 
 
 def body(token_ids, embed_table, norm_gain, client_gate, client_up, ref_gate, ref_up):
     normed = embed_norm(token_ids, norm_gain, embed_table)
-    token_count = normed.shape[0]
-    inverse_tokens = 1.0 / token_count
-    gate_local = jnp.dot(normed, client_gate[0], preferred_element_type=jnp.float32)
-    up_local = jnp.dot(normed, client_up[0], preferred_element_type=jnp.float32)
-    client_std = standardize(jax.nn.silu(gate_local) * up_local)
-    row_span = ref_gate.shape[0]
-    normed_slice = lax.dynamic_slice_in_dim(
-        normed, lax.axis_index("client") * row_span, row_span, 1
-    )
-    gate_part = jnp.dot(normed_slice, ref_gate, preferred_element_type=jnp.float32)
-    up_part = jnp.dot(normed_slice, ref_up, preferred_element_type=jnp.float32)
-    gate_share, up_share = sent_together((gate_part, up_part), "client", 1, 0)
-    ref_piece = standardize(jax.nn.silu(gate_share) * up_share)
-    ref_std = gather_directly(ref_piece, "client", 1)
-    local_units = client_std.shape[1]
-    segment = lax.all_gather(client_std, "unit", axis=1, tiled=True)
-    numerator = jnp.zeros((local_units, token_count), jnp.float32)
-    colsum = jnp.zeros((local_units,), jnp.float32)
-    weighted = jnp.zeros((local_units,), jnp.float32)
-    for offset, width in block_ranges(segment.shape[1]):
-        columns = segment[:, offset : offset + width]
-        correlation = (
-            jnp.dot(columns.T, ref_std, preferred_element_type=jnp.float32) * inverse_tokens
-        )
-        weights = jnp.exp(sharpness * correlation)
-        numerator = numerator + lax.dot_general(
-            weights.astype(jnp.bfloat16),
-            columns,
-            (((0,), (1,)), ((), ())),
-            preferred_element_type=jnp.float32,
-        )
-        colsum = colsum + jnp.sum(weights, axis=0)
-        weighted = weighted + jnp.sum(weights * correlation, axis=0)
-    numerator, colsum, weighted = (numerator, colsum, weighted)
-    matched = numerator / colsum[:, None]
-    score = (weighted / colsum)[None, :]
-    merged = nested_sum(matched.astype(jnp.bfloat16), "client") / lax.axis_size("client")
-    return (merged, score)
+    return aligned(normed, client_gate, client_up, ref_gate, ref_up)
 
 
 def solution(mesh):

time: 189 us -> 119 us (0.63)
  Pallas kernels: 36.3 us -> 108 us
  blocking collectives: 60.1 us -> 0 us
  waiting for transfers between devices: 39.9 us -> 0 us
  matrix products: 21.7 us -> 0 us
  between operations: 14.3 us -> 0.67 us
  starting transfers between devices: 4.78 us -> 0 us
  other arithmetic: 2.74 us -> 0 us
    pallas_call x0 -> x1, Pallas kernels: none -> 72.2 us  [aligned(): pl.pallas_call(align_kernel, out_shape=(jax.ShapeDtypeStruct((FF_HERE, TO...]
    all_to_all x3 -> x0, blocking collectives: 60.1 us -> none  [the longest x1 30 us: summed_on_arrival(): blocks = lax.all_to_all(split_up(shard, dim, count), axis, 0, 0, tiled=True)]
    all_gather x1 -> x0, waiting for transfers between devices: 31.5 us -> none  [body(): segment = lax.all_gather(client_std, 'unit', axis=1, tiled=True)]
    dot_general x12 -> x0, matrix products: 21.7 us -> none  [the longest x4 8.85 us: body(): jnp.dot(columns.T, ref_std, preferred_element_type=jnp.float32)]
    all_to_all x1 -> x0, waiting for transfers between devices: 8.36 us -> none  [copy_for_each(): return lax.all_to_all(copies, axis, split_axis=0, concat_axis=0, tiled=True)]
    all_to_all x1 -> x0, starting transfers between devices: 4.74 us -> none  [copy_for_each(): return lax.all_to_all(copies, axis, split_axis=0, concat_axis=0, tiled=True)]
    unnamed x16 -> x8, local copies, waits for them, and re-layouts: 2.94 us -> 7.65 us
  transfers between devices with their start and end apart: 2 -> 0, of which waited for: 2 -> 0; matrix products, arithmetic and copies ran while one was open for 2% -> 0% of each run, Pallas kernels for 0% -> 0%
where the time goes in v2:
time: 119 us; the launch traced here: 118 us
  Pallas kernels  108 us (91%)
  local copies, waits for them, and re-layouts  8.46 us (7%)
    pallas_call x1, Pallas kernels, aligned(): pl.pallas_call(align_kernel, out_shape=(jax.ShapeDtypeStruct((FF_HERE, TO...  72.2 us
    pallas_call x1, Pallas kernels, embed_norm(): pl.pallas_call(embed_kernel, out_shape=jax.ShapeDtypeStruct((TOK, D), bf)...  36.3 us
    unnamed x8, local copies, waits for them, and re-layouts  7.65 us

profile of v2, /device:TPU:17, one launch (start us, length us, event | category | flops | bytes accessed | tf_op | source)
XLA Modules:
  0.0 117.6 jit_solution(16906781632093884158)
XLA Ops:
  0.6 0.8 copy.9.ids_ref
  1.4 0.0 copy-start.1
  1.5 2.2 %copy-done.1 = bf16[512,4096]{1,0:T(8,128)(2,1)S(1)} copy-done((bf16[512,4096]{1,0:T(8,128)(2,1)S(1)}, bf16[512,4096]{1,0:T(8,128)(2,1)}, u32[]{:S(2)}) %copy-start.1) | copy-done | bytes 4194328
  3.6 0.0 copy-start.2
  3.6 0.7 copy-done.2
  4.4 36.3 %embed_norm.1.x_ref = bf16[256,4096]{1,0:T(8,128)(2,1)S(1)} custom-call(s32[256,1]{1,0:T(8,128)S(1)} %copy.9.ids_ref, f32[1,4096]{1,0:T(1,128)S(1)} %bitcast.2, bf16[512,4096]{1,0:T(8,128)(2,1)S(1)} %copy-done.1), custom_call_target="tpu_custom_call" | custom-call | tf_op jit(solution)/shard_map/embed_norm/pallas_call | solution.py:203
  40.6 0.0 copy-start
  40.6 1.3 %copy-done = bf16[256,4096]{1,0:T(8,128)(2,1)} copy-done((bf16[256,4096]{1,0:T(8,128)(2,1)}, bf16[256,4096]{1,0:T(8,128)(2,1)S(1)}, u32[]{:S(2)}) %copy-start) | copy-done | bytes 2097176
  42.0 72.2 %align.1 = (f32[896,256]{1,0:T(8,128)}, f32[1,896]{1,0:T(1,128)}) custom-call(bf16[256,4096]{1,0:T(8,128)(2,1)} %copy-done, bf16[1,4096,896]{2,1,0:T(8,128)(2,1)} %cg_ref.1, bf16[1,4096,896]{2,1,0:T(8,128)(2,1)} %cu_ref.1, bf16[256,896]{1,0:T(8,128)(2,1)} %rg_ref.1, bf16[256,896]{1,0:T(8,128)(2,1)} %ru_ref.1), custom_call_target="tpu_custom_call" | custom-call | tf_op jit(solution)/shard_map/align/pallas_call | solution.py:482
  114.2 2.2 %copy.12 = f32[896,256]{1,0:T(8,128)} copy(f32[896,256]{1,0:T(8,128)} %get-tuple-element.4) | data formatting | bytes 1835008
  116.4 1.3 %copy.13 = f32[1,896]{1,0:T(1,128)} copy(f32[1,896]{1,0:T(1,128)} %get-tuple-element.5) | data formatting | bytes 7168
Async XLA Ops:
  1.4 2.2 %copy-start.1 = (bf16[512,4096]{1,0:T(8,128)(2,1)S(1)}, bf16[512,4096]{1,0:T(8,128)(2,1)}, u32[]{:S(2)}) copy-start(bf16[512,4096]{1,0:T(8,128)(2,1)} %table_ref.1) | copy-start | bytes 12582916
  3.6 0.7 copy-start.2
  40.6 1.3 %copy-start = (bf16[256,4096]{1,0:T(8,128)(2,1)}, bf16[256,4096]{1,0:T(8,128)(2,1)S(1)}, u32[]{:S(2)}) copy-start(bf16[256,4096]{1,0:T(8,128)(2,1)S(1)} %embed_norm.1.x_ref) | copy-start | bytes 6291460

commit v3 on v1

v3 whole, which is shorter than its diff:
```python
import jax
import jax.numpy as jnp
from jax import lax
from jax.experimental import pallas as pl
from jax.experimental.pallas import tpu as pltpu
from jax.sharding import PartitionSpec as P

sharpness = 40.0
MESH = pl.DeviceIdType.MESH

TOK = 256
D = 4096
HALF = D // 2
PARTS = ((0, 640), (640, 640), (1280, 768))
ORDERS = ("xyz", "yzx", "zxy")


class Place:
    def __init__(self):
        client = lax.axis_index("client")
        unit = lax.axis_index("unit")
        self.core = client % 2
        self.x = (client // 2) % 4
        self.y = (unit % 2) * 2 + client // 8
        self.z = unit // 2

    def at(self, axis):
        return getattr(self, axis)

    def peer(self, axis, step):
        x, y, z, core = self.x, self.y, self.z, self.core
        if axis == "x":
            x = (x + step) % 4
        elif axis == "y":
            y = (y + step) % 4
        elif axis == "z":
            z = (z + step) % 4
        else:
            core = 1 - core
        return {"client": (y % 2) * 8 + x * 2 + core, "unit": z * 2 + y // 2}


    def plane_peer(self, dx, flip, hflip, cflip=0):
        x = (self.x + dx) % 4
        low = (self.y % 2 + flip) % 2
        high = (self.y // 2 + hflip) % 2
        return {"client": low * 8 + x * 2 + (self.core + cflip) % 2, "unit": self.z * 2 + high}

    def plane_piece(self, dx, flip):
        return ((self.x + dx) % 4) * 2 + (self.y % 2 + flip) % 2


def send(src, dst, ssem, rsem, peer):
    copy = pltpu.make_async_remote_copy(
        src_ref=src, dst_ref=dst, send_sem=ssem, recv_sem=rsem, device_id=peer, device_id_type=MESH
    )
    copy.start()
    return copy


def rows(start, size):
    return pl.ds(pl.multiple_of(start, size), size)

FF_HERE = 896
PIECE = 112
JOINT = 2 * FF_HERE
JC = 224
SHARES = (4, 3, 4, 4)
SPANS = ((0, 256), (256, 256), (512, 256), (768, 128))
RING8 = [(dx, f) for dx in range(4) for f in range(2)][1:]
CROSS = [(dx, f, c) for dx in range(4) for f in range(2) for c in range(2)][1:]
RING16 = [(dx, f, h) for h in range(2) for dx in range(4) for f in range(2)][1:]
EXP_SCALE = sharpness / TOK * 1.4426950408889634


def spread(h, axis):
    center = jnp.mean(h, axis=axis, keepdims=True)
    shifted = h - center
    width = jnp.sqrt(jnp.mean(shifted * shifted, axis=axis, keepdims=True) + 1e-06)
    return (shifted / width).astype(jnp.bfloat16)


def gated(g, u):
    return g / (1.0 + jnp.exp(-g)) * u


def kernel(ids_ref, gain_ref, table_ref, cg_ref, cu_ref, rg_ref, ru_ref, merged_ref, score_ref, *scratch):
    e = Refs(scratch)
    me = Place()
    core, other = me.core, 1 - me.core
    mate = me.peer("core", 1)
    client = lax.axis_index("client")
    ssem, rsem = e.ssem, e.rsem

    loads = []
    for k in range(6):
        p = k % 3
        off, width = PARTS[p]
        half = other if k < 3 else core
        at = pl.multiple_of(half * HALF + off, 128)
        load = pltpu.make_async_copy(table_ref.at[:, pl.ds(at, width)], e.tabs[k], e.tsem.at[k])
        load.start()
        loads.append(load)
        if k == 2:
            refload = []
            for t, src in enumerate((rg_ref, ru_ref)):
                load = pltpu.make_async_copy(src, e.rw.at[t], e.rwsem.at[t])
                load.start()
                refload.append(load)

    barrier = pltpu.get_barrier_semaphore()
    peers = [me.plane_peer(*r) for r in RING16] + [me.peer("z", d) for d in (1, 2, 3)] + [mate]
    peers += [me.plane_peer(dx, f, 0, 1) for dx, f in RING8]
    for peer in peers:
        pl.semaphore_signal(barrier, inc=1, device_id=peer, device_id_type=MESH)

    eye = lax.broadcasted_iota(jnp.int32, (128, 128), 0) == lax.broadcasted_iota(jnp.int32, (128, 128), 1)
    start = (client * 8 + lax.axis_index("unit")) * 512
    table_rows = (start + lax.broadcasted_iota(jnp.int32, (1, 512), 1)).astype(jnp.float32)
    for t in range(2):
        wide = ids_ref[:, pl.ds(t * 128, 128)].astype(jnp.float32)
        tall = jnp.sum(jnp.where(eye, wide, 0.0), axis=1, keepdims=True)
        e.pick[pl.ds(t * 128, 128), :] = jnp.where(tall == table_rows, 1.0, 0.0).astype(jnp.bfloat16)

    def looked_up(k):
        loads[k].wait()
        return jnp.dot(e.pick[...], e.tabs[k][...], preferred_element_type=jnp.float32).astype(jnp.bfloat16)

    sent = []
    for p in range(3):
        e.outs[p][...] = looked_up(p)
    pl.semaphore_wait(barrier, len(peers))
    for p in range(3):
        sent.append(send(e.outs[p], e.cins[p], ssem.at[p, 0, 0], rsem.at[p, 0, 0], mate))
    for p in range(3):
        e.accs[p][...] = looked_up(3 + p)
    wload = {}
    for q in range(3):
        for k, src in enumerate((cg_ref, cu_ref)):
            load = pltpu.make_async_copy(
                src.at[0, :, pl.ds(q * 256, 256)], e.w.at[q * 2 + k], e.wsem.at[q * 2 + k]
            )
            load.start()
            wload[q, k] = load
    for k, src in enumerate((cg_ref, cu_ref)):
        load = pltpu.make_async_copy(
            src.at[0, :, pl.ds(768, 128)], e.w.at[6, :, pl.ds(k * 128, 128)], e.wsem.at[6 + k]
        )
        load.start()
        wload[3, k] = load

    here = me.plane_piece(0, 0)
    depth = pl.ds(pl.multiple_of(client * 256, 256), 256)
    for t in range(2):
        refload[t].wait()
        e.rt[t] = e.rw[t].T
    e.wr[:, depth] = e.rt[core, rows(here * PIECE, PIECE), :]
    shared = []

    def share(count):
        for _ in range(count):
            n = len(shared)
            dx, f, c = CROSS[n]
            src = e.rt.at[(core + c) % 2, rows(me.plane_piece(dx, f) * PIECE, PIECE)]
            shared.append(send(src, e.wr.at[:, depth], e.ws_.at[n], e.wr_.at[n], me.plane_peer(dx, f, 0, c)))

    s1 = [[], [], []]
    for p in range(3):
        sent[p].wait()
        e.accs[p][...] = e.accs[p][...] + e.cins[p][...]
        axis = ORDERS[p][0]
        for d in (1, 2, 3):
            to = (me.at(axis) + d) % 4
            s1[p].append(
                send(e.accs[p].at[rows(to * 64, 64)], e.r1s[p].at[d - 1], ssem.at[p, 1, d - 1], rsem.at[p, 1, d - 1], me.peer(axis, d))
            )
    share(SHARES[0])
    s2 = [[], [], []]
    for p in range(3):
        for copy in s1[p]:
            copy.wait()
        own = e.accs[p][rows(me.at(ORDERS[p][0]) * 64, 64), :]
        e.a1s[p][...] = (own + e.r1s[p][0]) + (e.r1s[p][1] + e.r1s[p][2])
        axis = ORDERS[p][1]
        for d in (1, 2, 3):
            to = (me.at(axis) + d) % 4
            s2[p].append(
                send(e.a1s[p].at[rows(to * 16, 16)], e.r2s[p].at[d - 1], ssem.at[p, 2, d - 1], rsem.at[p, 2, d - 1], me.peer(axis, d))
            )
    share(SHARES[1])
    s3 = [[], [], []]
    for p in range(3):
        for copy in s2[p]:
            copy.wait()
        own = e.a1s[p][rows(me.at(ORDERS[p][1]) * 16, 16), :]
        e.a2s[p][...] = (own + e.r2s[p][0]) + (e.r2s[p][1] + e.r2s[p][2])
        axis = ORDERS[p][2]
        for d in (1, 2, 3):
            s3[p].append(
                send(e.a2s[p], e.r3s[p].at[d - 1], ssem.at[p, 3, d - 1], rsem.at[p, 3, d - 1], me.peer(axis, d))
            )
    share(SHARES[2])
    s4 = [[], [], []]
    for p in range(3):
        for copy in s3[p]:
            copy.wait()
        base = me.at(ORDERS[p][0]) * 64 + me.at(ORDERS[p][1]) * 16
        piece = e.fulls[p].at[core, rows(base, 16)]
        piece[...] = (e.a2s[p][...] + e.r3s[p][0]) + (e.r3s[p][1] + e.r3s[p][2])
        axis = ORDERS[p][1]
        for d in (1, 2, 3):
            s4[p].append(send(piece, piece, ssem.at[p, 4, d - 1], rsem.at[p, 4, d - 1], me.peer(axis, d)))
    share(SHARES[3])
    s5 = [[], [], []]
    s6 = [[], [], []]
    for p in range(3):
        for copy in s4[p]:
            copy.wait()
        axis = ORDERS[p][0]
        piece = e.fulls[p].at[core, rows(me.at(axis) * 64, 64)]
        for d in (1, 2, 3):
            s5[p].append(send(piece, piece, ssem.at[p, 5, d - 1], rsem.at[p, 5, d - 1], me.peer(axis, d)))
        s6[p].append(send(piece, piece, ssem.at[p, 6, 0], rsem.at[p, 6, 0], mate))
    for p in range(3):
        axis = ORDERS[p][0]
        for d in (1, 2, 3):
            s5[p][d - 1].wait()
            came = (me.at(axis) + 4 - d) % 4
            piece = e.fulls[p].at[core, rows(came * 64, 64)]
            s6[p].append(send(piece, piece, ssem.at[p, 6, d], rsem.at[p, 6, d], mate))
    for p in range(3):
        for copy in s6[p]:
            copy.wait()
    for t in range(0, TOK, 32):
        total = jnp.zeros((32, 1), jnp.float32)
        for p in range(3):
            for h in range(2):
                v = e.fulls[p][h, pl.ds(t, 32), :].astype(jnp.float32)
                total = total + jnp.sum(v * v, axis=1, keepdims=True)
        scale = lax.rsqrt(total * (1.0 / D) + 1e-05)
        for p, (off, width) in enumerate(PARTS):
            for h in range(2):
                v = e.fulls[p][h, pl.ds(t, 32), :].astype(jnp.float32)
                cols = pl.ds(h * HALF + off, width)
                e.x[pl.ds(t, 32), cols] = (v * scale * gain_ref[:, cols]).astype(jnp.bfloat16)

    for copy in shared:
        copy.wait()
    e.swap[...] = lax.dot_general(e.wr[...], e.x[...], (((1,), (1,)), ((), ())), preferred_element_type=jnp.float32)
    c3 = send(e.swap, e.swin, e.csem.at[1], e.crsem.at[1], mate)

    zcopies = []

    def client_block(q):
        start, width = SPANS[q]
        for k in range(2):
            wload[q, k].wait()
        if q < 3:
            g = jnp.dot(e.x[...], e.w[q * 2], preferred_element_type=jnp.float32)
            u = jnp.dot(e.x[...], e.w[q * 2 + 1], preferred_element_type=jnp.float32)
        else:
            both = jnp.dot(e.x[...], e.w[6], preferred_element_type=jnp.float32)
            g, u = both[:, :128], both[:, 128:]
        cols = pl.ds(start, width)
        e.units[0, :, cols] = spread(gated(g, u), 0)
        mine = e.units.at[0, :, cols]
        zcopies.append((
            send(mine, e.units.at[1, :, cols], e.zs.at[0, q], e.zr.at[0, q], me.peer("z", 1)),
            send(mine, e.units.at[3, :, cols], e.zs.at[1, q], e.zr.at[1, q], me.peer("z", 3)),
        ))

    relays = []

    def relay(q):
        cols = pl.ds(*SPANS[q])
        if q in (0, 3):
            zcopies[q][0].wait_recv()
            relays.append(send(e.units.at[1, :, cols], e.units.at[2, :, cols], e.zs.at[2, q], e.zr.at[2, q], me.peer("z", 1)))
        else:
            zcopies[q][1].wait_recv()
            relays.append(send(e.units.at[3, :, cols], e.units.at[2, :, cols], e.zs.at[2, q], e.zr.at[2, q], me.peer("z", 3)))

    client_block(0)
    c3.wait()
    mine = e.swap[...]
    theirs = e.swin[...]
    lead = core == 0
    g = jnp.where(lead, mine, theirs)
    u = jnp.where(lead, theirs, mine)
    high = me.y // 2
    piece_rows = rows(high * FF_HERE + here * PIECE, PIECE)
    half = pl.ds(pl.multiple_of(core * 128, 128), 128)
    piece_std = spread(gated(g, u), 1)
    e.refs[piece_rows, half] = jnp.where(lead, piece_std[:, :128], piece_std[:, 128:])
    piece = e.refs.at[piece_rows, half]
    for n, (dx, f, h) in enumerate(RING16, 1):
        send(piece, piece, e.xs.at[1, n], e.xr.at[1, n], me.plane_peer(dx, f, h))

    client_block(1)
    client_block(2)
    client_block(3)
    relay(0)
    relay(1)

    def ref_arrived(block):
        hop = (block + high) % 2
        for dx in range(4):
            for f in range(2):
                n = hop * 8 + dx * 2 + f

                def arrive():
                    pltpu.make_async_remote_copy(
                        src_ref=piece, dst_ref=piece, send_sem=e.xs.at[1, n], recv_sem=e.xr.at[1, n],
                        device_id=me.plane_peer(dx, f, hop), device_id_type=MESH,
                    ).wait()

                if dx == 0 and f == 0:
                    pl.when(hop != 0)(arrive)
                else:
                    arrive()
        part = e.refs.at[pl.ds(block * FF_HERE, FF_HERE), half]
        return send(part, part, e.csem.at[2 + block], e.crsem.at[2 + block], mate)

    def align(slot, first, block):
        @pl.loop(0, FF_HERE // JC)
        def _(t):
            js = rows(block * FF_HERE + t * JC, JC)
            r = e.refs[js, :]
            a = jnp.zeros((JC, 128), jnp.float32) if first else e.cs[js, :]
            b = jnp.zeros((JC, 128), jnp.float32) if first else e.ws[js, :]
            for start, width in SPANS:
                s = jnp.dot(r, e.units[slot, :, pl.ds(start, width)], preferred_element_type=jnp.float32)
                v = jnp.exp2(s * EXP_SCALE)
                e.wts[:, pl.ds(start, width)] = v.astype(jnp.bfloat16)
                vs = v * s
                for o in range(0, width, 128):
                    a = a + v[:, o : o + 128]
                    b = b + vs[:, o : o + 128]
            e.cs[js, :] = a
            e.ws[js, :] = b
            got = lax.dot_general(
                e.wts[...], e.units[slot], (((1,), (1,)), ((), ())), preferred_element_type=jnp.float32
            )
            e.num[js, :] = got if first else e.num[js, :] + got

    def to_row(v):
        return jnp.sum(jnp.where(eye, jnp.sum(v, axis=1, keepdims=True), 0.0), axis=0, keepdims=True)

    def join_start(block):
        for q in range(7):
            js = pl.ds(block * FF_HERE + q * 128, 128)
            e.col[block, pl.ds(q, 1), :] = to_row(e.cs[js, :])
            e.col[block, pl.ds(q + 8, 1), :] = to_row(e.ws[js, :])
        return send(e.col.at[block], e.colin.at[block], e.csem.at[4 + block], e.crsem.at[4 + block], me.peer("y", 2))

    def normalize(block):
        for q in range(7):
            js = pl.ds(block * FF_HERE + q * 128, 128)
            inv = 1.0 / (e.col[block, pl.ds(q, 1), :] + e.colin[block, pl.ds(q, 1), :])
            inv = jnp.sum(jnp.where(eye, inv, 0.0), axis=1, keepdims=True)
            n = (e.num[js, :] * inv).astype(jnp.bfloat16)
            e.nout[0, js, :] = n[:, :128]
            e.nout[1, js, :] = n[:, 128:]
        bs = pl.ds(block * FF_HERE, FF_HERE)
        return send(e.nout.at[other, bs], e.nin.at[bs], e.csem.at[6 + block], e.crsem.at[6 + block], mate)

    def plane_copy(block, dx, f):
        hop = (block + high) % 2
        n = hop * 8 + dx * 2 + f
        src = e.nsum.at[rows(block * FF_HERE + me.plane_piece(dx, f) * PIECE, PIECE)]
        return pltpu.make_async_remote_copy(
            src_ref=src, dst_ref=e.f2.at[n], send_sem=e.xs.at[2, n], recv_sem=e.xr.at[2, n],
            device_id=me.plane_peer(dx, f, hop), device_id_type=MESH,
        ), hop

    def reduce_start(block):
        bs = pl.ds(block * FF_HERE, FF_HERE)
        e.nsum[bs, :] = e.nout[core, bs, :] + e.nin[bs, :]
        for dx in range(4):
            for f in range(2):
                copy, hop = plane_copy(block, dx, f)
                if dx == 0 and f == 0:
                    pl.when(hop != 0)(copy.start)
                else:
                    copy.start()

    c5 = ref_arrived(0)
    relay(2)
    c5.wait()
    align(0, True, 0)
    relay(3)
    c5 = ref_arrived(1)
    for slot, way, forwarded in ((1, 0, (0, 3)), (3, 1, (1, 2))):
        for q in range(4):
            if q not in forwarded:
                zcopies[q][way].wait_recv()
        align(slot, False, 0)
    for copy in relays:
        copy.wait_recv()
    align(2, False, 0)
    c6 = join_start(0)
    c5.wait()
    align(0, True, 1)
    align(1, False, 1)
    c6.wait()
    c7 = normalize(0)
    align(3, False, 1)
    c7.wait()
    reduce_start(0)
    align(2, False, 1)
    c6 = join_start(1)
    c6.wait()
    c7 = normalize(1)
    for q in range(7):
        below = e.col[high, pl.ds(q, 1), :] + e.colin[high, pl.ds(q, 1), :]
        above = e.col[high, pl.ds(q + 8, 1), :] + e.colin[high, pl.ds(q + 8, 1), :]
        score_ref[:, pl.ds(q * 128, 128)] = above / below * (1.0 / TOK)
    c7.wait()
    reduce_start(1)
    total = e.nsum[piece_rows, :].astype(jnp.float32)
    for block in range(2):
        for dx in range(4):
            for f in range(2):
                copy, hop = plane_copy(block, dx, f)
                if dx == 0 and f == 0:
                    pl.when(hop != 0)(copy.wait)
                else:
                    copy.wait()
    for n in range(1, 16):
        total = total + e.f2[n].astype(jnp.float32)
    mine = e.fin.at[core, here]
    mine[...] = total.astype(jnp.bfloat16)
    c9 = []
    c10 = [send(mine, mine, e.csem.at[8], e.crsem.at[8], mate)]
    for n, (dx, f) in enumerate(RING8):
        c9.append(send(mine, mine, e.xs.at[3, n], e.xr.at[3, n], me.plane_peer(dx, f, 0)))
    for n, (dx, f) in enumerate(RING8):
        c9[n].wait()
        came = e.fin.at[core, me.plane_piece(4 - dx, f)]
        c10.append(send(came, came, e.csem.at[9 + n], e.crsem.at[9 + n], mate))
    for copy in c10:
        copy.wait()
    for s in range(8):
        for h in range(2):
            merged_ref[pl.ds(s * PIECE, PIECE), pl.ds(h * 128, 128)] = e.fin[h, s].astype(jnp.float32) * (1.0 / 16)
    for pair in zcopies:
        pair[0].wait_send()
        pair[1].wait_send()
    for copy in relays:
        copy.wait_send()


def layout():
    bf, f32 = jnp.bfloat16, jnp.float32
    dma = pltpu.SemaphoreType.DMA
    vm = pltpu.VMEM
    widths = [w for _, w in PARTS]
    return {
        "tabs": [vm((512, w), bf) for w in widths * 2],
        "accs": [vm((TOK, w), bf) for w in widths],
        "outs": [vm((TOK, w), bf) for w in widths],
        "cins": [vm((TOK, w), bf) for w in widths],
        "r1s": [vm((3, 64, w), bf) for w in widths],
        "a1s": [vm((64, w), bf) for w in widths],
        "r2s": [vm((3, 16, w), bf) for w in widths],
        "a2s": [vm((16, w), bf) for w in widths],
        "r3s": [vm((3, 16, w), bf) for w in widths],
        "fulls": [vm((2, TOK, w), bf) for w in widths],
        "pick": vm((TOK, 512), bf),
        "x": vm((TOK, D), bf),
        "w": vm((7, D, 256), bf),
        "rw": vm((2, 256, FF_HERE), bf),
        "rt": vm((2, FF_HERE, 256), bf),
        "wr": vm((PIECE, D), bf),
        "swap": vm((PIECE, TOK), f32),
        "swin": vm((PIECE, TOK), f32),
        "refs": vm((JOINT, TOK), bf),
        "units": vm((4, TOK, FF_HERE), bf),
        "wts": vm((JC, FF_HERE), bf),
        "num": vm((JOINT, TOK), f32),
        "cs": vm((JOINT, 128), f32),
        "ws": vm((JOINT, 128), f32),
        "col": vm((2, 16, 128), f32),
        "colin": vm((2, 16, 128), f32),
        "nout": vm((2, JOINT, 128), bf),
        "nin": vm((JOINT, 128), bf),
        "nsum": vm((JOINT, 128), bf),
        "f2": vm((16, PIECE, 128), bf),
        "fin": vm((2, 8, PIECE, 128), bf),
        "tsem": dma((6,)),
        "ssem": dma((3, 7, 4)),
        "rsem": dma((3, 7, 4)),
        "wsem": dma((8,)),
        "rwsem": dma((2,)),
        "ws_": dma((15,)),
        "wr_": dma((15,)),
        "csem": dma((16,)),
        "crsem": dma((16,)),
        "zs": dma((3, 4)),
        "zr": dma((3, 4)),
        "xs": dma((4, 16)),
        "xr": dma((4, 16)),
    }


class Refs:
    def __init__(self, scratch):
        left = list(scratch)
        for name, shape in layout().items():
            if isinstance(shape, list):
                setattr(self, name, [left.pop(0) for _ in shape])
            else:
                setattr(self, name, left.pop(0))


def body(token_ids, embed_table, norm_gain, client_gate, client_up, ref_gate, ref_up):
    shapes = []
    for shape in layout().values():
        shapes += shape if isinstance(shape, list) else [shape]
    vmem = pl.BlockSpec(memory_space=pltpu.VMEM)
    hbm = pl.BlockSpec(memory_space=pl.ANY)
    return pl.pallas_call(
        kernel,
        out_shape=(
            jax.ShapeDtypeStruct((FF_HERE, TOK), jnp.float32),
            jax.ShapeDtypeStruct((1, FF_HERE), jnp.float32),
        ),
        in_specs=[vmem, vmem, hbm, hbm, hbm, hbm, hbm],
        out_specs=(vmem, vmem),
        scratch_shapes=shapes,
        compiler_params=pltpu.CompilerParams(collective_id=0, has_side_effects=True, vmem_limit_bytes=60 << 20),
        name="soft_alignment",
    )(token_ids[None, :], norm_gain[None, :], embed_table, client_gate, client_up, ref_gate, ref_up)


def solution(mesh):
    in_specs = (
        P(),
        P(("client", "unit"), None),
        P(),
        P("client", None, "unit"),
        P("client", None, "unit"),
        P("client", "unit"),
        P("client", "unit"),
    )
    out_specs = (P("unit", None), P("client", "unit"))
    return jax.shard_map(body, mesh=mesh, in_specs=in_specs, out_specs=out_specs, check_vma=False)
```

time: 189 us -> 101 us (0.53); the launches traced: 187 us -> 101 us
  Pallas kernels: 36.3 us -> 96.8 us
  blocking collectives: 60.1 us -> 0 us
  waiting for transfers between devices: 39.9 us -> 0 us
  matrix products: 21.7 us -> 0 us
  between operations: 14.3 us -> 0.64 us
  starting transfers between devices: 4.78 us -> 0 us
  local copies, waits for them, and re-layouts: 6.97 us -> 3.41 us
  other arithmetic: 2.74 us -> 0 us
    pallas_call x1, Pallas kernels: 36.3 us -> 96.8 us  [body(): pl.pallas_call(kernel, out_shape=(jax.ShapeDtypeStruct((FF_HERE, TOK), jn...]
    all_to_all x3 -> x0, blocking collectives: 60.1 us -> none  [the longest x1 30 us: summed_on_arrival(): blocks = lax.all_to_all(split_up(shard, dim, count), axis, 0, 0, tiled=True)]
    all_gather x1 -> x0, waiting for transfers between devices: 31.5 us -> none  [body(): segment = lax.all_gather(client_std, 'unit', axis=1, tiled=True)]
    dot_general x12 -> x0, matrix products: 21.7 us -> none  [the longest x4 8.85 us: body(): jnp.dot(columns.T, ref_std, preferred_element_type=jnp.float32)]
    all_to_all x1 -> x0, waiting for transfers between devices: 8.36 us -> none  [copy_for_each(): return lax.all_to_all(copies, axis, split_axis=0, concat_axis=0, tiled=True)]
    all_to_all x1 -> x0, starting transfers between devices: 4.74 us -> none  [copy_for_each(): return lax.all_to_all(copies, axis, split_axis=0, concat_axis=0, tiled=True)]
  transfers between devices with their start and end apart: 2 -> 0, of which waited for: 2 -> 0; matrix products, arithmetic and copies ran while one was open for 2% -> 0% of each run, Pallas kernels for 0% -> 0%
where the time goes in v3:
time: 101 us
  Pallas kernels  96.8 us (96%)
  local copies, waits for them, and re-layouts  3.41 us (3%)
    pallas_call x1, Pallas kernels, body(): pl.pallas_call(kernel, out_shape=(jax.ShapeDtypeStruct((FF_HERE, TOK), jn...  96.8 us
    unnamed x2, local copies, waits for them, and re-layouts  3.41 us

profile of v3, /device:TPU:17, one launch (start us, length us, event | category | flops | bytes accessed | tf_op | source)
XLA Modules:
  0.0 100.9 jit_solution(14332324061018383195)
XLA Ops:
  0.6 96.8 %soft_alignment.1 = (f32[896,256]{1,0:T(8,128)}, f32[1,896]{1,0:T(1,128)}) custom-call(s32[1,256]{1,0:T(1,128)} %bitcast.3, f32[1,4096]{1,0:T(1,128)} %bitcast.2, bf16[512,4096]{1,0:T(8,128)(2,1)} %table_ref.1, bf16[1,4096,896]{2,1,0:T(8,128)(2,1)} %cg_ref.1, bf16[1,4096,896]{2,1,0:T(8,128)(2,1)} %cu_ref.1, bf16[256,896]{1,0:T(8,128)(2,1)} %rg_ref.1, ...), custom_call_target="tpu_custom_call" | custom-call | tf_op jit(solution)/shard_map/soft_alignment/pallas_call | solution.py:522
  97.5 2.2 %copy.11 = f32[896,256]{1,0:T(8,128)} copy(f32[896,256]{1,0:T(8,128)} %get-tuple-element.4) | data formatting | bytes 1835008
  99.6 1.3 %copy.12 = f32[1,896]{1,0:T(1,128)} copy(f32[1,896]{1,0:T(1,128)} %get-tuple-element.5) | data formatting | bytes 7168

commit v4 on v3

--- a/solution.py
+++ b/solution.py
@@ -11,8 +11,9 @@
 TOK = 256
 D = 4096
 HALF = D // 2
-PARTS = ((0, 640), (640, 640), (1280, 768))
-ORDERS = ("xyz", "yzx", "zxy")
+PARTS = ((0, 384), (384, 384), (768, 384), (1152, 384), (1536, 256), (1792, 256))
+ORDERS = ("xyz", "yzx", "zxy") * 2
+NP = len(PARTS)
 
 
 class Place:
@@ -64,8 +65,8 @@
 FF_HERE = 896
 PIECE = 112
 JOINT = 2 * FF_HERE
-JC = 224
-SHARES = (4, 3, 4, 4)
+JC = 896
+SHARES = (6, 0, 5, 4)
 SPANS = ((0, 256), (256, 256), (512, 256), (768, 128))
 RING8 = [(dx, f) for dx in range(4) for f in range(2)][1:]
 CROSS = [(dx, f, c) for dx in range(4) for f in range(2) for c in range(2)][1:]
@@ -92,21 +93,19 @@
     client = lax.axis_index("client")
     ssem, rsem = e.ssem, e.rsem
 
+    refload = []
+    for t, src in enumerate((rg_ref, ru_ref)):
+        load = pltpu.make_async_copy(src, e.rw.at[t], e.rwsem.at[t])
+        load.start()
+        refload.append(load)
     loads = []
-    for k in range(6):
-        p = k % 3
-        off, width = PARTS[p]
-        half = other if k < 3 else core
+    for k in range(2 * NP):
+        off, width = PARTS[k % NP]
+        half = other if k < NP else core
         at = pl.multiple_of(half * HALF + off, 128)
         load = pltpu.make_async_copy(table_ref.at[:, pl.ds(at, width)], e.tabs[k], e.tsem.at[k])
         load.start()
         loads.append(load)
-        if k == 2:
-            refload = []
-            for t, src in enumerate((rg_ref, ru_ref)):
-                load = pltpu.make_async_copy(src, e.rw.at[t], e.rwsem.at[t])
-                load.start()
-                refload.append(load)
 
     barrier = pltpu.get_barrier_semaphore()
     peers = [me.plane_peer(*r) for r in RING16] + [me.peer("z", d) for d in (1, 2, 3)] + [mate]
@@ -126,14 +125,29 @@
         loads[k].wait()
         return jnp.dot(e.pick[...], e.tabs[k][...], preferred_element_type=jnp.float32).astype(jnp.bfloat16)
 
+    here = me.plane_piece(0, 0)
+    depth = pl.ds(pl.multiple_of(client * 256, 256), 256)
+    for t in range(2):
+        refload[t].wait()
+        e.rt[t] = e.rw[t].T
+    e.wr[:, depth] = e.rt[core, rows(here * PIECE, PIECE), :]
+    shared = []
+
+    def share(count):
+        for _ in range(count):
+            n = len(shared)
+            dx, f, c = CROSS[n]
+            src = e.rt.at[(core + c) % 2, rows(me.plane_piece(dx, f) * PIECE, PIECE)]
+            shared.append(send(src, e.wr.at[:, depth], e.ws_.at[n], e.wr_.at[n], me.plane_peer(dx, f, 0, c)))
+
+    pl.semaphore_wait(barrier, len(peers))
+    share(SHARES[0])
     sent = []
-    for p in range(3):
+    for p in range(NP):
         e.outs[p][...] = looked_up(p)
-    pl.semaphore_wait(barrier, len(peers))
-    for p in range(3):
         sent.append(send(e.outs[p], e.cins[p], ssem.at[p, 0, 0], rsem.at[p, 0, 0], mate))
-    for p in range(3):
-        e.accs[p][...] = looked_up(3 + p)
+    for p in range(NP):
+        e.accs[p][...] = looked_up(NP + p)
     wload = {}
     for q in range(3):
         for k, src in enumerate((cg_ref, cu_ref)):
@@ -149,23 +163,8 @@
         load.start()
         wload[3, k] = load
 
-    here = me.plane_piece(0, 0)
-    depth = pl.ds(pl.multiple_of(client * 256, 256), 256)
-    for t in range(2):
-        refload[t].wait()
-        e.rt[t] = e.rw[t].T
-    e.wr[:, depth] = e.rt[core, rows(here * PIECE, PIECE), :]
-    shared = []
-
-    def share(count):
-        for _ in range(count):
-            n = len(shared)
-            dx, f, c = CROSS[n]
-            src = e.rt.at[(core + c) % 2, rows(me.plane_piece(dx, f) * PIECE, PIECE)]
-            shared.append(send(src, e.wr.at[:, depth], e.ws_.at[n], e.wr_.at[n], me.plane_peer(dx, f, 0, c)))
-
-    s1 = [[], [], []]
-    for p in range(3):
+    s1 = [[] for _ in range(NP)]
+    for p in range(NP):
         sent[p].wait()
         e.accs[p][...] = e.accs[p][...] + e.cins[p][...]
         axis = ORDERS[p][0]
@@ -174,9 +173,8 @@
             s1[p].append(
                 send(e.accs[p].at[rows(to * 64, 64)], e.r1s[p].at[d - 1], ssem.at[p, 1, d - 1], rsem.at[p, 1, d - 1], me.peer(axis, d))
             )
-    share(SHARES[0])
-    s2 = [[], [], []]
-    for p in range(3):
+    s2 = [[] for _ in range(NP)]
+    for p in range(NP):
         for copy in s1[p]:
             copy.wait()
         own = e.accs[p][rows(me.at(ORDERS[p][0]) * 64, 64), :]
@@ -188,8 +186,8 @@
                 send(e.a1s[p].at[rows(to * 16, 16)], e.r2s[p].at[d - 1], ssem.at[p, 2, d - 1], rsem.at[p, 2, d - 1], me.peer(axis, d))
             )
     share(SHARES[1])
-    s3 = [[], [], []]
-    for p in range(3):
+    s3 = [[] for _ in range(NP)]
+    for p in range(NP):
         for copy in s2[p]:
             copy.wait()
         own = e.a1s[p][rows(me.at(ORDERS[p][1]) * 16, 16), :]
@@ -200,8 +198,8 @@
                 send(e.a2s[p], e.r3s[p].at[d - 1], ssem.at[p, 3, d - 1], rsem.at[p, 3, d - 1], me.peer(axis, d))
             )
     share(SHARES[2])
-    s4 = [[], [], []]
-    for p in range(3):
+    s4 = [[] for _ in range(NP)]
+    for p in range(NP):
         for copy in s3[p]:
             copy.wait()
         base = me.at(ORDERS[p][0]) * 64 + me.at(ORDERS[p][1]) * 16
@@ -211,9 +209,9 @@
         for d in (1, 2, 3):
             s4[p].append(send(piece, piece, ssem.at[p, 4, d - 1], rsem.at[p, 4, d - 1], me.peer(axis, d)))
     share(SHARES[3])
-    s5 = [[], [], []]
-    s6 = [[], [], []]
-    for p in range(3):
+    s5 = [[] for _ in range(NP)]
+    s6 = [[] for _ in range(NP)]
+    for p in range(NP):
         for copy in s4[p]:
             copy.wait()
         axis = ORDERS[p][0]
@@ -221,19 +219,19 @@
         for d in (1, 2, 3):
             s5[p].append(send(piece, piece, ssem.at[p, 5, d - 1], rsem.at[p, 5, d - 1], me.peer(axis, d)))
         s6[p].append(send(piece, piece, ssem.at[p, 6, 0], rsem.at[p, 6, 0], mate))
-    for p in range(3):
+    for p in range(NP):
         axis = ORDERS[p][0]
         for d in (1, 2, 3):
             s5[p][d - 1].wait()
             came = (me.at(axis) + 4 - d) % 4
             piece = e.fulls[p].at[core, rows(came * 64, 64)]
             s6[p].append(send(piece, piece, ssem.at[p, 6, d], rsem.at[p, 6, d], mate))
-    for p in range(3):
+    for p in range(NP):
         for copy in s6[p]:
             copy.wait()
     for t in range(0, TOK, 32):
         total = jnp.zeros((32, 1), jnp.float32)
-        for p in range(3):
+        for p in range(NP):
             for h in range(2):
                 v = e.fulls[p][h, pl.ds(t, 32), :].astype(jnp.float32)
                 total = total + jnp.sum(v * v, axis=1, keepdims=True)
@@ -243,11 +241,6 @@
                 v = e.fulls[p][h, pl.ds(t, 32), :].astype(jnp.float32)
                 cols = pl.ds(h * HALF + off, width)
                 e.x[pl.ds(t, 32), cols] = (v * scale * gain_ref[:, cols]).astype(jnp.bfloat16)
-
-    for copy in shared:
-        copy.wait()
-    e.swap[...] = lax.dot_general(e.wr[...], e.x[...], (((1,), (1,)), ((), ())), preferred_element_type=jnp.float32)
-    c3 = send(e.swap, e.swin, e.csem.at[1], e.crsem.at[1], mate)
 
     zcopies = []
 
@@ -281,6 +274,12 @@
             relays.append(send(e.units.at[3, :, cols], e.units.at[2, :, cols], e.zs.at[2, q], e.zr.at[2, q], me.peer("z", 3)))
 
     client_block(0)
+    for copy in shared:
+        copy.wait()
+    e.swap[...] = lax.dot_general(e.wr[...], e.x[...], (((1,), (1,)), ((), ())), preferred_element_type=jnp.float32)
+    c3 = send(e.swap, e.swin, e.csem.at[1], e.crsem.at[1], mate)
+
+    client_block(1)
     c3.wait()
     mine = e.swap[...]
     theirs = e.swin[...]
@@ -293,14 +292,16 @@
     piece_std = spread(gated(g, u), 1)
     e.refs[piece_rows, half] = jnp.where(lead, piece_std[:, :128], piece_std[:, 128:])
     piece = e.refs.at[piece_rows, half]
-    for n, (dx, f, h) in enumerate(RING16, 1):
-        send(piece, piece, e.xs.at[1, n], e.xr.at[1, n], me.plane_peer(dx, f, h))
-
-    client_block(1)
+
+    def hand_out():
+        for n, (dx, f, h) in enumerate(RING16, 1):
+            send(piece, piece, e.xs.at[1, n], e.xr.at[1, n], me.plane_peer(dx, f, h))
+
+    pl.when(high == 0)(hand_out)
     client_block(2)
     client_block(3)
+    pl.when(high == 1)(hand_out)
     relay(0)
-    relay(1)
 
     def ref_arrived(block):
         hop = (block + high) % 2
@@ -385,30 +386,32 @@
                     copy.start()
 
     c5 = ref_arrived(0)
-    relay(2)
+    relay(1)
     c5.wait()
     align(0, True, 0)
+    relay(2)
+    c5 = ref_arrived(1)
     relay(3)
-    c5 = ref_arrived(1)
-    for slot, way, forwarded in ((1, 0, (0, 3)), (3, 1, (1, 2))):
+    c5.wait()
+    align(0, True, 1)
+    for way, forwarded in ((0, (0, 3)), (1, (1, 2))):
         for q in range(4):
             if q not in forwarded:
                 zcopies[q][way].wait_recv()
-        align(slot, False, 0)
+    align(1, False, 0)
+    align(3, False, 0)
+    align(1, False, 1)
+    align(3, False, 1)
     for copy in relays:
         copy.wait_recv()
     align(2, False, 0)
     c6 = join_start(0)
-    c5.wait()
-    align(0, True, 1)
-    align(1, False, 1)
+    align(2, False, 1)
     c6.wait()
     c7 = normalize(0)
-    align(3, False, 1)
+    c6 = join_start(1)
     c7.wait()
     reduce_start(0)
-    align(2, False, 1)
-    c6 = join_start(1)
     c6.wait()
     c7 = normalize(1)
     for q in range(7):
@@ -487,9 +490,9 @@
         "nsum": vm((JOINT, 128), bf),
         "f2": vm((16, PIECE, 128), bf),
         "fin": vm((2, 8, PIECE, 128), bf),
-        "tsem": dma((6,)),
-        "ssem": dma((3, 7, 4)),
-        "rsem": dma((3, 7, 4)),
+        "tsem": dma((2 * NP,)),
+        "ssem": dma((NP, 7, 4)),
+        "rsem": dma((NP, 7, 4)),
         "wsem": dma((8,)),
         "rwsem": dma((2,)),
         "ws_": dma((15,)),

time: 101 us -> 99 us (0.980)
  Pallas kernels: 96.8 us -> 94.7 us
    pallas_call x1, Pallas kernels: 96.8 us -> 94.7 us  [body(): pl.pallas_call(kernel, out_shape=(jax.ShapeDtypeStruct((FF_HERE, TOK), jn...]
where the time goes in v4:
time: 99 us; the launch traced here: 98.7 us
  Pallas kernels  94.7 us (96%)
  local copies, waits for them, and re-layouts  3.41 us (3%)
    pallas_call x1, Pallas kernels, body(): pl.pallas_call(kernel, out_shape=(jax.ShapeDtypeStruct((FF_HERE, TOK), jn...  94.7 us
    unnamed x2, local copies, waits for them, and re-layouts  3.41 us

profile of v4, /device:TPU:17, one launch (start us, length us, event | category | flops | bytes accessed | tf_op | source)
XLA Modules:
  0.0 98.7 jit_solution(4797131302017317782)
XLA Ops:
  0.6 94.7 %soft_alignment.1 = (f32[896,256]{1,0:T(8,128)}, f32[1,896]{1,0:T(1,128)}) custom-call(s32[1,256]{1,0:T(1,128)} %bitcast.3, f32[1,4096]{1,0:T(1,128)} %bitcast.2, bf16[512,4096]{1,0:T(8,128)(2,1)} %table_ref.1, bf16[1,4096,896]{2,1,0:T(8,128)(2,1)} %cg_ref.1, bf16[1,4096,896]{2,1,0:T(8,128)(2,1)} %cu_ref.1, bf16[256,896]{1,0:T(8,128)(2,1)} %rg_ref.1, ...), custom_call_target="tpu_custom_call" | custom-call | tf_op jit(solution)/shard_map/soft_alignment/pallas_call | solution.py:525
  95.3 2.2 %copy.11 = f32[896,256]{1,0:T(8,128)} copy(f32[896,256]{1,0:T(8,128)} %get-tuple-element.4) | data formatting | bytes 1835008
  97.5 1.3 %copy.12 = f32[1,896]{1,0:T(1,128)} copy(f32[1,896]{1,0:T(1,128)} %get-tuple-element.5) | data formatting | bytes 7168

commit v5 on v4

v5 whole, which is shorter than its diff:
```python
import jax
import jax.numpy as jnp
from jax import lax
from jax.experimental import pallas as pl
from jax.experimental.pallas import tpu as pltpu
from jax.sharding import PartitionSpec as P

sharpness = 40.0
MESH = pl.DeviceIdType.MESH

TOK = 256
D = 4096
HALF = D // 2
PARTS = ((0, 384), (384, 384), (768, 384), (1152, 384), (1536, 256), (1792, 256))
ORDERS = ("xyz", "yzx", "zxy") * 2
NP = len(PARTS)


class Place:
    def __init__(self):
        client = lax.axis_index("client")
        unit = lax.axis_index("unit")
        self.core = client % 2
        self.x = (client // 2) % 4
        self.y = (unit % 2) * 2 + client // 8
        self.z = unit // 2

    def at(self, axis):
        return getattr(self, axis)

    def peer(self, axis, step):
        x, y, z, core = self.x, self.y, self.z, self.core
        if axis == "x":
            x = (x + step) % 4
        elif axis == "y":
            y = (y + step) % 4
        elif axis == "z":
            z = (z + step) % 4
        else:
            core = 1 - core
        return {"client": (y % 2) * 8 + x * 2 + core, "unit": z * 2 + y // 2}


    def plane_peer(self, dx, flip, hflip, cflip=0):
        x = (self.x + dx) % 4
        low = (self.y % 2 + flip) % 2
        high = (self.y // 2 + hflip) % 2
        return {"client": low * 8 + x * 2 + (self.core + cflip) % 2, "unit": self.z * 2 + high}

    def plane_piece(self, dx, flip):
        return ((self.x + dx) % 4) * 2 + (self.y % 2 + flip) % 2


def send(src, dst, ssem, rsem, peer):
    copy = pltpu.make_async_remote_copy(
        src_ref=src, dst_ref=dst, send_sem=ssem, recv_sem=rsem, device_id=peer, device_id_type=MESH
    )
    copy.start()
    return copy


def drain(sem, ref):
    pltpu.make_async_copy(ref, ref, sem).wait()


def rows(start, size):
    return pl.ds(pl.multiple_of(start, size), size)

FF_HERE = 896
PIECE = 112
JOINT = 2 * FF_HERE
JC = 896
SHARES = (5, 3, 4, 3)
SPANS = ((0, 256), (256, 256), (512, 256), (768, 128))
RING8 = [(dx, f) for dx in range(4) for f in range(2)][1:]
CROSS = [(dx, f, c) for dx in range(4) for f in range(2) for c in range(2)][1:]
RING16 = [(dx, f, h) for h in range(2) for dx in range(4) for f in range(2)][1:]
EXP_SCALE = sharpness / TOK * 1.4426950408889634


def spread(h, axis):
    center = jnp.mean(h, axis=axis, keepdims=True)
    shifted = h - center
    width = jnp.sqrt(jnp.mean(shifted * shifted, axis=axis, keepdims=True) + 1e-06)
    return (shifted / width).astype(jnp.bfloat16)


def gated(g, u):
    return g / (1.0 + jnp.exp(-g)) * u


def kernel(ids_ref, gain_ref, table_ref, cg_ref, cu_ref, rg_ref, ru_ref, fin_ref, score_ref, *scratch):
    e = Refs(scratch)
    me = Place()
    core, other = me.core, 1 - me.core
    mate = me.peer("core", 1)
    client = lax.axis_index("client")
    ssem, rsem = e.ssem, e.rsem

    def table_load(k):
        half = other if k < 4 else core
        at = pl.multiple_of(half * HALF + k % 4 * 512, 512)
        load = pltpu.make_async_copy(table_ref.at[:, pl.ds(at, 512)], e.tabs.at[k], e.tsem.at[k])
        load.start()
        return load

    loads = [table_load(k) for k in range(8)]
    for t, src in enumerate((rg_ref, ru_ref)):
        pltpu.make_async_copy(src, e.rw.at[t], e.rwsem.at[0]).start()

    barrier = pltpu.get_barrier_semaphore()
    peers = [me.plane_peer(*r) for r in RING16] + [me.peer("z", d) for d in (1, 2, 3)] + [mate]
    peers += [me.plane_peer(dx, f, 0, 1) for dx, f in RING8]
    for peer in peers:
        pl.semaphore_signal(barrier, inc=1, device_id=peer, device_id_type=MESH)

    eye = lax.broadcasted_iota(jnp.int32, (128, 128), 0) == lax.broadcasted_iota(jnp.int32, (128, 128), 1)
    start = (client * 8 + lax.axis_index("unit")) * 512
    table_rows = (start + lax.broadcasted_iota(jnp.int32, (1, 512), 1)).astype(jnp.float32)
    for t in range(2):
        wide = ids_ref[:, pl.ds(t * 128, 128)].astype(jnp.float32)
        tall = jnp.sum(jnp.where(eye, wide, 0.0), axis=1, keepdims=True)
        e.pick[pl.ds(t * 128, 128), :] = jnp.where(tall == table_rows, 1.0, 0.0).astype(jnp.bfloat16)

    def looked_up(k):
        loads[k].wait()
        return jnp.dot(e.pick[...], e.tabs[k], preferred_element_type=jnp.float32).astype(jnp.bfloat16)

    chunks = [pl.ds(k * 512, 512) for k in range(4)]
    for k in range(4):
        e.outs[:, chunks[k]] = looked_up(k)
    pl.semaphore_wait(barrier, len(peers))
    sent = []
    for k in range(4):
        sent.append(send(e.outs.at[:, chunks[k]], e.cins.at[:, chunks[k]], e.csem.at[0], e.crsem.at[k], mate))
    for k in range(4):
        e.accs[:, chunks[k]] = looked_up(4 + k)
    wload = {}
    for q in range(3):
        for k, src in enumerate((cg_ref, cu_ref)):
            load = pltpu.make_async_copy(
                src.at[0, :, pl.ds(q * 256, 256)], e.w.at[q * 2 + k], e.wsem.at[q * 2 + k]
            )
            load.start()
            wload[q, k] = load
    for k, src in enumerate((cg_ref, cu_ref)):
        load = pltpu.make_async_copy(
            src.at[0, :, pl.ds(768, 128)], e.w.at[6, :, pl.ds(k * 128, 128)], e.wsem.at[6 + k]
        )
        load.start()
        wload[3, k] = load

    for k in range(4):
        sent[k].wait_recv()
        e.accs[:, chunks[k]] = e.accs[:, chunks[k]] + e.cins[:, chunks[k]]
    for p in range(NP):
        axis = ORDERS[p][0]
        for d in (1, 2, 3):
            to = (me.at(axis) + d) % 4
            src = e.accs.at[rows(to * 64, 64), pl.ds(*PARTS[p])]
            send(src, e.r1s[p].at[d - 1], ssem.at[p], rsem.at[p, 0], me.peer(axis, d))

    here = me.plane_piece(0, 0)
    depth = pl.ds(pl.multiple_of(client * 256, 256), 256)
    drain(e.rwsem.at[0], e.rw)
    for t in range(2):
        e.rt[t] = e.rw[t].T
    e.wr[:, depth] = e.rt[core, rows(here * PIECE, PIECE), :]
    shared = []

    def share(count):
        for _ in range(count):
            n = len(shared)
            dx, f, c = CROSS[n]
            src = e.rt.at[(core + c) % 2, rows(me.plane_piece(dx, f) * PIECE, PIECE)]
            shared.append(send(src, e.wr.at[:, depth], e.wshare.at[0], e.wshare.at[1], me.plane_peer(dx, f, 0, c)))

    share(SHARES[0])
    for p in range(NP):
        drain(rsem.at[p, 0], e.r1s[p])
        drain(ssem.at[p], e.r1s[p])
        own = e.accs[rows(me.at(ORDERS[p][0]) * 64, 64), pl.ds(*PARTS[p])]
        e.a1s[p][...] = (own + e.r1s[p][0]) + (e.r1s[p][1] + e.r1s[p][2])
        axis = ORDERS[p][1]
        for d in (1, 2, 3):
            to = (me.at(axis) + d) % 4
            send(e.a1s[p].at[rows(to * 16, 16)], e.r2s[p].at[d - 1], ssem.at[p], rsem.at[p, 1], me.peer(axis, d))
    drain(e.csem.at[0], e.outs)
    share(SHARES[1])
    for p in range(NP):
        drain(rsem.at[p, 1], e.r2s[p])
        drain(ssem.at[p], e.r2s[p])
        own = e.a1s[p][rows(me.at(ORDERS[p][1]) * 16, 16), :]
        e.a2s[p][...] = (own + e.r2s[p][0]) + (e.r2s[p][1] + e.r2s[p][2])
        axis = ORDERS[p][2]
        for d in (1, 2, 3):
            send(e.a2s[p], e.r3s[p].at[d - 1], ssem.at[p], rsem.at[p, 2], me.peer(axis, d))
    share(SHARES[2])
    for p in range(NP):
        drain(rsem.at[p, 2], e.r3s[p])
        drain(ssem.at[p], e.r3s[p])
        base = me.at(ORDERS[p][0]) * 64 + me.at(ORDERS[p][1]) * 16
        piece = e.fulls[p].at[core, rows(base, 16)]
        piece[...] = (e.a2s[p][...] + e.r3s[p][0]) + (e.r3s[p][1] + e.r3s[p][2])
        axis = ORDERS[p][1]
        for d in (1, 2, 3):
            send(piece, piece, ssem.at[p], rsem.at[p, 3], me.peer(axis, d))
    share(SHARES[3])
    for p in range(NP):
        drain(rsem.at[p, 3], e.r2s[p])
        drain(ssem.at[p], e.r2s[p])
        axis = ORDERS[p][0]
        piece = e.fulls[p].at[core, rows(me.at(axis) * 64, 64)]
        for d in (1, 2, 3):
            send(piece, piece, ssem.at[p], rsem.at[p, 4], me.peer(axis, d))
    s6 = []
    for p in range(NP):
        drain(rsem.at[p, 4], e.r1s[p])
        drain(ssem.at[p], e.r1s[p])
        piece = e.fulls[p].at[core]
        s6.append(send(piece, piece, ssem.at[p], rsem.at[p, 5], mate))
    for p in range(NP):
        s6[p].wait()
    for t in range(0, TOK, 32):
        total = jnp.zeros((32, 1), jnp.float32)
        for p in range(NP):
            for h in range(2):
                v = e.fulls[p][h, pl.ds(t, 32), :].astype(jnp.float32)
                total = total + jnp.sum(v * v, axis=1, keepdims=True)
        scale = lax.rsqrt(total * (1.0 / D) + 1e-05)
        for p, (off, width) in enumerate(PARTS):
            for h in range(2):
                v = e.fulls[p][h, pl.ds(t, 32), :].astype(jnp.float32)
                cols = pl.ds(h * HALF + off, width)
                e.x[pl.ds(t, 32), cols] = (v * scale * gain_ref[:, cols]).astype(jnp.bfloat16)

    def client_block(q):
        start, width = SPANS[q]
        for k in range(2):
            wload[q, k].wait()
        if q < 3:
            g = jnp.dot(e.x[...], e.w[q * 2], preferred_element_type=jnp.float32)
            u = jnp.dot(e.x[...], e.w[q * 2 + 1], preferred_element_type=jnp.float32)
        else:
            both = jnp.dot(e.x[...], e.w[6], preferred_element_type=jnp.float32)
            g, u = both[:, :128], both[:, 128:]
        cols = pl.ds(start, width)
        e.units[0, :, cols] = spread(gated(g, u), 0)
        mine = e.units.at[0, :, cols]
        send(mine, e.units.at[1, :, cols], e.zs.at[0], e.zr.at[(0, 2, 2, 1)[q]], me.peer("z", 1))
        send(mine, e.units.at[3, :, cols], e.zs.at[0], e.zr.at[(5, 3, 4, 5)[q]], me.peer("z", 3))

    def relay(q):
        slot, step = (1, 1) if q in (0, 3) else (3, 3)
        piece = e.units.at[slot, :, pl.ds(*SPANS[q])]
        drain(e.zr.at[(0, 3, 4, 1)[q]], piece)
        send(piece, e.units.at[2, :, pl.ds(*SPANS[q])], e.zs.at[1], e.zr.at[6], me.peer("z", step))

    client_block(0)
    drain(e.wshare.at[0], e.wr.at[:, pl.ds(256, D - 256)])
    drain(e.wshare.at[1], e.wr.at[:, pl.ds(256, D - 256)])
    e.swap[...] = lax.dot_general(e.wr[...], e.x[...], (((1,), (1,)), ((), ())), preferred_element_type=jnp.float32)
    c3 = send(e.swap, e.swin, e.csem.at[1], e.crsem.at[4], mate)

    client_block(1)
    c3.wait()
    mine = e.swap[...]
    theirs = e.swin[...]
    lead = core == 0
    g = jnp.where(lead, mine, theirs)
    u = jnp.where(lead, theirs, mine)
    high = me.y // 2
    piece_rows = rows(high * FF_HERE + here * PIECE, PIECE)
    half = pl.ds(pl.multiple_of(core * 128, 128), 128)
    piece_std = spread(gated(g, u), 1)
    e.refs[piece_rows, half] = jnp.where(lead, piece_std[:, :128], piece_std[:, 128:])
    piece = e.refs.at[piece_rows, half]

    for dx, f in RING8:
        send(piece, piece, e.xs.at[0], e.xr.at[0], me.plane_peer(dx, f, 0))
    send(piece, piece, e.xs.at[1], e.xr.at[1], me.plane_peer(0, 0, 1))
    client_block(2)
    client_block(3)
    piece = e.refs.at[rows((1 - high) * FF_HERE + here * PIECE, PIECE), half]
    drain(e.xr.at[1], piece)
    drain(e.xs.at[1], piece)
    for dx, f in RING8:
        send(piece, piece, e.xs.at[1], e.xr.at[2], me.plane_peer(dx, f, 0))

    def ref_arrived(k):
        seven = e.refs.at[pl.ds(0, 7 * PIECE), half]
        drain(e.xr.at[(0, 2)[k]], seven)
        drain(e.xs.at[k], seven)
        block = high if k == 0 else 1 - high
        part = e.refs.at[rows(block * FF_HERE, FF_HERE), half]
        return send(part, part, e.csem.at[2 + k], e.crsem.at[5 + k], mate)

    def align(slot, first, block):
        @pl.loop(0, FF_HERE // JC)
        def _(t):
            js = rows(block * FF_HERE + t * JC, JC)
            r = e.refs[js, :]
            a = jnp.zeros((JC, 128), jnp.float32) if first else e.cs[js, :]
            b = jnp.zeros((JC, 128), jnp.float32) if first else e.ws[js, :]
            for start, width in SPANS:
                s = jnp.dot(r, e.units[slot, :, pl.ds(start, width)], preferred_element_type=jnp.float32)
                v = jnp.exp2(s * EXP_SCALE)
                e.wts[:, pl.ds(start, width)] = v.astype(jnp.bfloat16)
                vs = v * s
                for o in range(0, width, 128):
                    a = a + v[:, o : o + 128]
                    b = b + vs[:, o : o + 128]
            e.cs[js, :] = a
            e.ws[js, :] = b
            got = lax.dot_general(
                e.wts[...], e.units[slot], (((1,), (1,)), ((), ())), preferred_element_type=jnp.float32
            )
            e.num[js, :] = got if first else e.num[js, :] + got

    def to_row(v):
        return jnp.sum(jnp.where(eye, jnp.sum(v, axis=1, keepdims=True), 0.0), axis=0, keepdims=True)

    def join_start():
        for block in range(2):
            for q in range(7):
                js = pl.ds(block * FF_HERE + q * 128, 128)
                e.col[block, pl.ds(q, 1), :] = to_row(e.cs[js, :])
                e.col[block, pl.ds(q + 8, 1), :] = to_row(e.ws[js, :])
        return send(e.col, e.colin, e.csem.at[4], e.crsem.at[7], me.peer("y", 2))

    def normalize(block):
        for q in range(7):
            js = pl.ds(block * FF_HERE + q * 128, 128)
            inv = 1.0 / (e.col[block, pl.ds(q, 1), :] + e.colin[block, pl.ds(q, 1), :])
            inv = jnp.sum(jnp.where(eye, inv, 0.0), axis=1, keepdims=True)
            n = (e.num[js, :] * inv).astype(jnp.bfloat16)
            e.nout[0, js, :] = n[:, :128]
            e.nout[1, js, :] = n[:, 128:]
        bs = pl.ds(block * FF_HERE, FF_HERE)
        return send(e.nout.at[other, bs], e.nin.at[bs], e.csem.at[5 + block], e.crsem.at[8 + block], mate)

    def reduce_start(block):
        bs = pl.ds(block * FF_HERE, FF_HERE)
        e.nsum[bs, :] = e.nout[core, bs, :] + e.nin[bs, :]
        hop = (block + high) % 2
        for dx in range(4):
            for f in range(2):
                n = hop * 8 + dx * 2 + f
                src = e.nsum.at[rows(block * FF_HERE + me.plane_piece(dx, f) * PIECE, PIECE)]
                copy = pltpu.make_async_remote_copy(
                    src_ref=src, dst_ref=e.f2.at[n], send_sem=e.xs.at[2], recv_sem=e.xr.at[3],
                    device_id=me.plane_peer(dx, f, hop), device_id_type=MESH,
                )
                if dx == 0 and f == 0:
                    pl.when(hop != 0)(copy.start)
                else:
                    copy.start()

    c5 = ref_arrived(0)
    relay(0)
    c5.wait()
    align(0, True, high)
    relay(1)
    c5 = ref_arrived(1)
    relay(2)
    c5.wait()
    align(0, True, 1 - high)
    relay(3)
    drain(e.zr.at[2], e.units.at[1, :, pl.ds(256, 512)])
    align(1, False, 0)
    align(1, False, 1)
    drain(e.zr.at[5], e.units.at[3, :, pl.ds(0, 384)])
    align(3, False, 0)
    align(3, False, 1)
    drain(e.zr.at[6], e.units.at[2])
    align(2, False, 0)
    align(2, False, 1)
    c6 = join_start()
    c6.wait()
    c7 = [normalize(0), normalize(1)]
    for q in range(7):
        below = e.col[high, pl.ds(q, 1), :] + e.colin[high, pl.ds(q, 1), :]
        above = e.col[high, pl.ds(q + 8, 1), :] + e.colin[high, pl.ds(q + 8, 1), :]
        score_ref[:, pl.ds(q * 128, 128)] = above / below * (1.0 / TOK)
    for block in range(2):
        c7[block].wait()
        reduce_start(block)
    drain(e.xr.at[3], e.f2.at[pl.ds(1, 15)])
    drain(e.xs.at[2], e.f2.at[pl.ds(1, 15)])
    total = e.nsum[piece_rows, :].astype(jnp.float32)
    for n in range(1, 16):
        total = total + e.f2[n].astype(jnp.float32)
    mine = e.fin.at[core, here]
    mine[...] = total.astype(jnp.bfloat16)
    for dx, f in RING8:
        send(mine, mine, e.xs.at[3], e.xr.at[4], me.plane_peer(dx, f, 0))
    drain(e.xr.at[4], e.fin.at[0, pl.ds(1, 7)])
    drain(e.xs.at[3], e.fin.at[0, pl.ds(1, 7)])
    c10 = send(e.fin.at[core], e.fin.at[core], e.csem.at[7], e.crsem.at[10], mate)
    for _ in range(2):
        drain(e.zs.at[0], e.units.at[0])
    drain(e.zs.at[1], e.units.at[2])
    c10.wait()
    fin_ref[...] = e.fin[...]


def finish_kernel(fin_ref, mean_ref, merged_ref, score_ref):
    for s in range(8):
        for h in range(2):
            merged_ref[pl.ds(s * PIECE, PIECE), pl.ds(h * 128, 128)] = fin_ref[h, s].astype(jnp.float32) * (1.0 / 16)
    score_ref[...] = mean_ref[...]


def layout():
    bf, f32 = jnp.bfloat16, jnp.float32
    dma = pltpu.SemaphoreType.DMA
    vm = pltpu.VMEM
    widths = [w for _, w in PARTS]
    return {
        "tabs": vm((8, 512, 512), bf),
        "accs": vm((TOK, HALF), bf),
        "outs": vm((TOK, HALF), bf),
        "cins": vm((TOK, HALF), bf),
        "r1s": [vm((3, 64, w), bf) for w in widths],
        "a1s": [vm((64, w), bf) for w in widths],
        "r2s": [vm((3, 16, w), bf) for w in widths],
        "a2s": [vm((16, w), bf) for w in widths],
        "r3s": [vm((3, 16, w), bf) for w in widths],
        "fulls": [vm((2, TOK, w), bf) for w in widths],
        "pick": vm((TOK, 512), bf),
        "x": vm((TOK, D), bf),
        "w": vm((7, D, 256), bf),
        "rw": vm((2, 256, FF_HERE), bf),
        "rt": vm((2, FF_HERE, 256), bf),
        "wr": vm((PIECE, D), bf),
        "swap": vm((PIECE, TOK), f32),
        "swin": vm((PIECE, TOK), f32),
        "refs": vm((JOINT, TOK), bf),
        "units": vm((4, TOK, FF_HERE), bf),
        "wts": vm((JC, FF_HERE), bf),
        "num": vm((JOINT, TOK), f32),
        "cs": vm((JOINT, 128), f32),
        "ws": vm((JOINT, 128), f32),
        "col": vm((2, 16, 128), f32),
        "colin": vm((2, 16, 128), f32),
        "nout": vm((2, JOINT, 128), bf),
        "nin": vm((JOINT, 128), bf),
        "nsum": vm((JOINT, 128), bf),
        "f2": vm((16, PIECE, 128), bf),
        "fin": vm((2, 8, PIECE, 128), bf),
        "tsem": dma((8,)),
        "ssem": dma((NP,)),
        "rsem": dma((NP, 6)),
        "wsem": dma((8,)),
        "rwsem": dma((1,)),
        "wshare": dma((2,)),
        "csem": dma((8,)),
        "crsem": dma((11,)),
        "zs": dma((2,)),
        "zr": dma((7,)),
        "xs": dma((4,)),
        "xr": dma((5,)),
    }


class Refs:
    def __init__(self, scratch):
        left = list(scratch)
        for name, shape in layout().items():
            if isinstance(shape, list):
                setattr(self, name, [left.pop(0) for _ in shape])
            else:
                setattr(self, name, left.pop(0))


def body(token_ids, embed_table, norm_gain, client_gate, client_up, ref_gate, ref_up):
    shapes = []
    for shape in layout().values():
        shapes += shape if isinstance(shape, list) else [shape]
    vmem = pl.BlockSpec(memory_space=pltpu.VMEM)
    hbm = pl.BlockSpec(memory_space=pl.ANY)
    f32 = jnp.float32
    fin, mean = pl.pallas_call(
        kernel,
        out_shape=(
            jax.ShapeDtypeStruct((2, 8, PIECE, 128), jnp.bfloat16),
            jax.ShapeDtypeStruct((1, FF_HERE), f32),
        ),
        in_specs=[vmem, vmem, hbm, hbm, hbm, hbm, hbm],
        out_specs=(vmem, vmem),
        scratch_shapes=shapes,
        compiler_params=pltpu.CompilerParams(collective_id=0, has_side_effects=True, vmem_limit_bytes=60 << 20),
        name="soft_alignment",
    )(token_ids[None, :], norm_gain[None, :], embed_table, client_gate, client_up, ref_gate, ref_up)
    return pl.pallas_call(
        finish_kernel,
        out_shape=(jax.ShapeDtypeStruct((FF_HERE, TOK), f32), jax.ShapeDtypeStruct((1, FF_HERE), f32)),
        in_specs=[vmem, vmem],
        out_specs=(vmem, vmem),
        name="finish",
    )(fin, mean)


def solution(mesh):
    in_specs = (
        P(),
        P(("client", "unit"), None),
        P(),
        P("client", None, "unit"),
        P("client", None, "unit"),
        P("client", "unit"),
        P("client", "unit"),
    )
    out_specs = (P("unit", None), P("client", "unit"))
    return jax.shard_map(body, mesh=mesh, in_specs=in_specs, out_specs=out_specs, check_vma=False)
```

time: 99 us -> 88.6 us (0.89)
  Pallas kernels: 94.7 us -> 87.5 us
  local copies, waits for them, and re-layouts: 3.41 us -> 0 us
    pallas_call x1 -> x2, Pallas kernels: 94.7 us -> 87.5 us  [the longest x1 85.5 us: body(): pl.pallas_call(kernel, out_shape=(jax.ShapeDtypeStruct((2, 8, PIECE, 128)...]
    unnamed x2 -> x0, local copies, waits for them, and re-layouts: 3.41 us -> none
where the time goes in v5:
time: 88.6 us; the launch traced here: 88.2 us
  Pallas kernels  87.5 us (99%)
    pallas_call x1, Pallas kernels, body(): pl.pallas_call(kernel, out_shape=(jax.ShapeDtypeStruct((2, 8, PIECE, 128)...  85.5 us
    pallas_call x1, Pallas kernels, body(): pl.pallas_call(finish_kernel, out_shape=(jax.ShapeDtypeStruct((FF_HERE, T...  2.01 us

profile of v5, /device:TPU:17, one launch (start us, length us, event | category | flops | bytes accessed | tf_op | source)
XLA Modules:
  0.0 88.2 jit_solution(8750095932633216814)
XLA Ops:
  0.6 85.5 %soft_alignment.1 = (bf16[2,8,112,128]{3,2,1,0:T(8,128)(2,1)}, f32[1,896]{1,0:T(1,128)}) custom-call(s32[1,256]{1,0:T(1,128)} %bitcast.3, f32[1,4096]{1,0:T(1,128)} %bitcast.2, bf16[512,4096]{1,0:T(8,128)(2,1)} %table_ref.1, bf16[1,4096,896]{2,1,0:T(8,128)(2,1)} %cg_ref.1, bf16[1,4096,896]{2,1,0:T(8,128)(2,1)} %cu_ref.1, bf16[256,896]{1,0:T(8,128)(2,1)} %rg_ref.1, ...), custom_call_target="tpu_custom_call" | custom-call | tf_op jit(solution)/shard_map/soft_alignment/pallas_call | solution.py:483
  86.1 2.0 %finish.1 = (f32[896,256]{1,0:T(8,128)}, f32[1,896]{1,0:T(1,128)}) custom-call(bf16[2,8,112,128]{3,2,1,0:T(8,128)(2,1)} %get-tuple-element.4.fin_ref, f32[1,896]{1,0:T(1,128)} %get-tuple-element.5.mean_ref), custom_call_target="tpu_custom_call" | custom-call | tf_op jit(solution)/shard_map/finish/pallas_call | solution.py:495

commit v6 on v5

--- a/solution.py
+++ b/solution.py
@@ -69,8 +69,7 @@
 FF_HERE = 896
 PIECE = 112
 JOINT = 2 * FF_HERE
-JC = 896
-SHARES = (5, 3, 4, 3)
+SHARES = (4, 3, 3, 3, 2, 0)
 SPANS = ((0, 256), (256, 256), (512, 256), (768, 128))
 RING8 = [(dx, f) for dx in range(4) for f in range(2)][1:]
 CROSS = [(dx, f, c) for dx in range(4) for f in range(2) for c in range(2)][1:]
@@ -104,9 +103,10 @@
         load.start()
         return load
 
-    loads = [table_load(k) for k in range(8)]
+    loads = [table_load(k) for k in range(4)]
     for t, src in enumerate((rg_ref, ru_ref)):
         pltpu.make_async_copy(src, e.rw.at[t], e.rwsem.at[0]).start()
+    loads += [table_load(k) for k in range(4, 8)]
 
     barrier = pltpu.get_barrier_semaphore()
     peers = [me.plane_peer(*r) for r in RING16] + [me.peer("z", d) for d in (1, 2, 3)] + [mate]
@@ -129,10 +129,26 @@
     chunks = [pl.ds(k * 512, 512) for k in range(4)]
     for k in range(4):
         e.outs[:, chunks[k]] = looked_up(k)
+    here = me.plane_piece(0, 0)
+    depth = pl.ds(pl.multiple_of(client * 256, 256), 256)
+    drain(e.rwsem.at[0], e.rw)
+    for t in range(2):
+        e.rt[t] = e.rw[t].T
+    e.wr[:, depth] = e.rt[core, rows(here * PIECE, PIECE), :]
+    shared = []
+
+    def share(count):
+        for _ in range(count):
+            n = len(shared)
+            dx, f, c = CROSS[n]
+            src = e.rt.at[(core + c) % 2, rows(me.plane_piece(dx, f) * PIECE, PIECE)]
+            shared.append(send(src, e.wr.at[:, depth], e.wshare.at[0], e.wshare.at[1], me.plane_peer(dx, f, 0, c)))
+
     pl.semaphore_wait(barrier, len(peers))
     sent = []
     for k in range(4):
         sent.append(send(e.outs.at[:, chunks[k]], e.cins.at[:, chunks[k]], e.csem.at[0], e.crsem.at[k], mate))
+    share(SHARES[0])
     for k in range(4):
         e.accs[:, chunks[k]] = looked_up(4 + k)
     wload = {}
@@ -160,22 +176,7 @@
             src = e.accs.at[rows(to * 64, 64), pl.ds(*PARTS[p])]
             send(src, e.r1s[p].at[d - 1], ssem.at[p], rsem.at[p, 0], me.peer(axis, d))
 
-    here = me.plane_piece(0, 0)
-    depth = pl.ds(pl.multiple_of(client * 256, 256), 256)
-    drain(e.rwsem.at[0], e.rw)
-    for t in range(2):
-        e.rt[t] = e.rw[t].T
-    e.wr[:, depth] = e.rt[core, rows(here * PIECE, PIECE), :]
-    shared = []
-
-    def share(count):
-        for _ in range(count):
-            n = len(shared)
-            dx, f, c = CROSS[n]
-            src = e.rt.at[(core + c) % 2, rows(me.plane_piece(dx, f) * PIECE, PIECE)]
-            shared.append(send(src, e.wr.at[:, depth], e.wshare.at[0], e.wshare.at[1], me.plane_peer(dx, f, 0, c)))
-
-    share(SHARES[0])
+    share(SHARES[1])
     for p in range(NP):
         drain(rsem.at[p, 0], e.r1s[p])
         drain(ssem.at[p], e.r1s[p])
@@ -186,7 +187,7 @@
             to = (me.at(axis) + d) % 4
             send(e.a1s[p].at[rows(to * 16, 16)], e.r2s[p].at[d - 1], ssem.at[p], rsem.at[p, 1], me.peer(axis, d))
     drain(e.csem.at[0], e.outs)
-    share(SHARES[1])
+    share(SHARES[2])
     for p in range(NP):
         drain(rsem.at[p, 1], e.r2s[p])
         drain(ssem.at[p], e.r2s[p])
@@ -195,7 +196,7 @@
         axis = ORDERS[p][2]
         for d in (1, 2, 3):
             send(e.a2s[p], e.r3s[p].at[d - 1], ssem.at[p], rsem.at[p, 2], me.peer(axis, d))
-    share(SHARES[2])
+    share(SHARES[3])
     for p in range(NP):
         drain(rsem.at[p, 2], e.r3s[p])
         drain(ssem.at[p], e.r3s[p])
@@ -205,7 +206,7 @@
         axis = ORDERS[p][1]
         for d in (1, 2, 3):
             send(piece, piece, ssem.at[p], rsem.at[p, 3], me.peer(axis, d))
-    share(SHARES[3])
+    share(SHARES[4])
     for p in range(NP):
         drain(rsem.at[p, 3], e.r2s[p])
         drain(ssem.at[p], e.r2s[p])
@@ -213,14 +214,35 @@
         piece = e.fulls[p].at[core, rows(me.at(axis) * 64, 64)]
         for d in (1, 2, 3):
             send(piece, piece, ssem.at[p], rsem.at[p, 4], me.peer(axis, d))
+    share(SHARES[5])
     s6 = []
     for p in range(NP):
         drain(rsem.at[p, 4], e.r1s[p])
         drain(ssem.at[p], e.r1s[p])
         piece = e.fulls[p].at[core]
         s6.append(send(piece, piece, ssem.at[p], rsem.at[p, 5], mate))
+    apart = e.wr.at[:, pl.ds(256, D - 256)]
+    drain(e.wshare.at[1], apart)
+    drain(e.wshare.at[0], apart)
+    for t in range(0, D, 512):
+        cols = pl.ds(t, 512)
+        e.wr[:, cols] = (e.wr[:, cols].astype(jnp.float32) * gain_ref[:, cols]).astype(jnp.bfloat16)
+
+    def ref_part(p, h):
+        off, width = PARTS[p]
+        cols = pl.ds(pl.multiple_of(h * HALF + off, 128), width)
+        return lax.dot_general(
+            e.wr[:, cols], e.fulls[p][h], (((1,), (1,)), ((), ())), preferred_element_type=jnp.float32
+        )
+
+    product = ref_part(0, core)
+    for p in range(1, NP):
+        product = product + ref_part(p, core)
     for p in range(NP):
         s6[p].wait()
+        product = product + ref_part(p, other)
+    e.swap[...] = product
+    c3 = send(e.swap, e.swin, e.csem.at[1], e.crsem.at[4], mate)
     for t in range(0, TOK, 32):
         total = jnp.zeros((32, 1), jnp.float32)
         for p in range(NP):
@@ -228,11 +250,33 @@
                 v = e.fulls[p][h, pl.ds(t, 32), :].astype(jnp.float32)
                 total = total + jnp.sum(v * v, axis=1, keepdims=True)
         scale = lax.rsqrt(total * (1.0 / D) + 1e-05)
+        e.scl[pl.ds(t, 32), :] = jnp.broadcast_to(scale, (32, 128))
         for p, (off, width) in enumerate(PARTS):
             for h in range(2):
                 v = e.fulls[p][h, pl.ds(t, 32), :].astype(jnp.float32)
                 cols = pl.ds(h * HALF + off, width)
                 e.x[pl.ds(t, 32), cols] = (v * scale * gain_ref[:, cols]).astype(jnp.bfloat16)
+
+    c3.wait()
+    scale_row = jnp.concatenate(
+        [jnp.sum(jnp.where(eye, e.scl[pl.ds(t, 128), :], 0.0), axis=0, keepdims=True) for t in (0, 128)], axis=1
+    )
+    mine = e.swap[...] * scale_row
+    theirs = e.swin[...] * scale_row
+    lead = core == 0
+    g = jnp.where(lead, mine, theirs)
+    u = jnp.where(lead, theirs, mine)
+    high = me.y // 2
+    piece_rows = rows(high * FF_HERE + here * PIECE, PIECE)
+    half = pl.ds(pl.multiple_of(core * 128, 128), 128)
+    piece_std = spread(gated(g, u), 1)
+    e.refs[piece_rows, half] = jnp.where(lead, piece_std[:, :128], piece_std[:, 128:])
+    piece = e.refs.at[piece_rows, half]
+    for dx, f in RING8:
+        send(piece, piece, e.xs.at[0], e.xr.at[0], me.plane_peer(dx, f, 0))
+    for dx in range(4):
+        for f in range(2):
+            send(piece, piece, e.xs.at[1], e.xr.at[2], me.plane_peer(dx, f, 1))
 
     def client_block(q):
         start, width = SPANS[q]
@@ -247,86 +291,62 @@
         cols = pl.ds(start, width)
         e.units[0, :, cols] = spread(gated(g, u), 0)
         mine = e.units.at[0, :, cols]
-        send(mine, e.units.at[1, :, cols], e.zs.at[0], e.zr.at[(0, 2, 2, 1)[q]], me.peer("z", 1))
-        send(mine, e.units.at[3, :, cols], e.zs.at[0], e.zr.at[(5, 3, 4, 5)[q]], me.peer("z", 3))
+        send(mine, e.units.at[1, :, cols], e.zs.at[0], e.zr.at[q], me.peer("z", 1))
+        send(mine, e.units.at[3, :, cols], e.zs.at[0], e.zr.at[8 + q], me.peer("z", 3))
 
     def relay(q):
         slot, step = (1, 1) if q in (0, 3) else (3, 3)
         piece = e.units.at[slot, :, pl.ds(*SPANS[q])]
-        drain(e.zr.at[(0, 3, 4, 1)[q]], piece)
-        send(piece, e.units.at[2, :, pl.ds(*SPANS[q])], e.zs.at[1], e.zr.at[6], me.peer("z", step))
+        drain(e.zr.at[q if slot == 1 else 8 + q], piece)
+        send(piece, e.units.at[2, :, pl.ds(*SPANS[q])], e.zs.at[1], e.zr.at[4 + q], me.peer("z", step))
+
+    def unit_wait(slot, q):
+        drain(e.zr.at[(slot - 1) * 4 + q], e.units.at[slot, :, pl.ds(*SPANS[q])])
 
     client_block(0)
-    drain(e.wshare.at[0], e.wr.at[:, pl.ds(256, D - 256)])
-    drain(e.wshare.at[1], e.wr.at[:, pl.ds(256, D - 256)])
-    e.swap[...] = lax.dot_general(e.wr[...], e.x[...], (((1,), (1,)), ((), ())), preferred_element_type=jnp.float32)
-    c3 = send(e.swap, e.swin, e.csem.at[1], e.crsem.at[4], mate)
-
     client_block(1)
-    c3.wait()
-    mine = e.swap[...]
-    theirs = e.swin[...]
-    lead = core == 0
-    g = jnp.where(lead, mine, theirs)
-    u = jnp.where(lead, theirs, mine)
-    high = me.y // 2
-    piece_rows = rows(high * FF_HERE + here * PIECE, PIECE)
-    half = pl.ds(pl.multiple_of(core * 128, 128), 128)
-    piece_std = spread(gated(g, u), 1)
-    e.refs[piece_rows, half] = jnp.where(lead, piece_std[:, :128], piece_std[:, 128:])
-    piece = e.refs.at[piece_rows, half]
-
-    for dx, f in RING8:
-        send(piece, piece, e.xs.at[0], e.xr.at[0], me.plane_peer(dx, f, 0))
-    send(piece, piece, e.xs.at[1], e.xr.at[1], me.plane_peer(0, 0, 1))
     client_block(2)
     client_block(3)
-    piece = e.refs.at[rows((1 - high) * FF_HERE + here * PIECE, PIECE), half]
-    drain(e.xr.at[1], piece)
-    drain(e.xs.at[1], piece)
-    for dx, f in RING8:
-        send(piece, piece, e.xs.at[1], e.xr.at[2], me.plane_peer(dx, f, 0))
-
     def ref_arrived(k):
-        seven = e.refs.at[pl.ds(0, 7 * PIECE), half]
-        drain(e.xr.at[(0, 2)[k]], seven)
-        drain(e.xs.at[k], seven)
+        came = e.refs.at[pl.ds(0, (7 + k) * PIECE), half]
+        drain(e.xr.at[(0, 2)[k]], came)
+        drain(e.xs.at[k], came)
         block = high if k == 0 else 1 - high
         part = e.refs.at[rows(block * FF_HERE, FF_HERE), half]
         return send(part, part, e.csem.at[2 + k], e.crsem.at[5 + k], mate)
 
-    def align(slot, first, block):
-        @pl.loop(0, FF_HERE // JC)
-        def _(t):
-            js = rows(block * FF_HERE + t * JC, JC)
-            r = e.refs[js, :]
-            a = jnp.zeros((JC, 128), jnp.float32) if first else e.cs[js, :]
-            b = jnp.zeros((JC, 128), jnp.float32) if first else e.ws[js, :]
-            for start, width in SPANS:
-                s = jnp.dot(r, e.units[slot, :, pl.ds(start, width)], preferred_element_type=jnp.float32)
-                v = jnp.exp2(s * EXP_SCALE)
-                e.wts[:, pl.ds(start, width)] = v.astype(jnp.bfloat16)
-                vs = v * s
-                for o in range(0, width, 128):
-                    a = a + v[:, o : o + 128]
-                    b = b + vs[:, o : o + 128]
-            e.cs[js, :] = a
-            e.ws[js, :] = b
-            got = lax.dot_general(
-                e.wts[...], e.units[slot], (((1,), (1,)), ((), ())), preferred_element_type=jnp.float32
-            )
-            e.num[js, :] = got if first else e.num[js, :] + got
+    def align(slot, block, k, first=False):
+        left, wide = ((0, 512), (512, 384))[k]
+        js = rows(block * FF_HERE, FF_HERE)
+        r = e.refs[js, :]
+        a = jnp.zeros((FF_HERE, 128), jnp.float32) if first else e.cs[js, :]
+        b = jnp.zeros((FF_HERE, 128), jnp.float32) if first else e.ws[js, :]
+        for start in range(0, wide, 256):
+            width = min(256, wide - start)
+            s = jnp.dot(r, e.units[slot, :, pl.ds(left + start, width)], preferred_element_type=jnp.float32)
+            v = jnp.exp2(s * EXP_SCALE)
+            e.wts[:, pl.ds(start, width)] = v.astype(jnp.bfloat16)
+            vs = v * s
+            for o in range(0, width, 128):
+                a = a + v[:, o : o + 128]
+                b = b + vs[:, o : o + 128]
+        e.cs[js, :] = a
+        e.ws[js, :] = b
+        got = lax.dot_general(
+            e.wts[:, pl.ds(0, wide)], e.units[slot, :, pl.ds(left, wide)], (((1,), (1,)), ((), ())),
+            preferred_element_type=jnp.float32,
+        )
+        e.num[js, :] = got if first else e.num[js, :] + got
 
     def to_row(v):
         return jnp.sum(jnp.where(eye, jnp.sum(v, axis=1, keepdims=True), 0.0), axis=0, keepdims=True)
 
-    def join_start():
-        for block in range(2):
-            for q in range(7):
-                js = pl.ds(block * FF_HERE + q * 128, 128)
-                e.col[block, pl.ds(q, 1), :] = to_row(e.cs[js, :])
-                e.col[block, pl.ds(q + 8, 1), :] = to_row(e.ws[js, :])
-        return send(e.col, e.colin, e.csem.at[4], e.crsem.at[7], me.peer("y", 2))
+    def join_start(block):
+        for q in range(7):
+            js = pl.ds(block * FF_HERE + q * 128, 128)
+            e.col[block, pl.ds(q, 1), :] = to_row(e.cs[js, :])
+            e.col[block, pl.ds(q + 8, 1), :] = to_row(e.ws[js, :])
+        return send(e.col.at[block], e.colin.at[block], e.jsem.at[block], e.jsem.at[2 + block], me.peer("y", 2))
 
     def normalize(block):
         for q in range(7):
@@ -359,32 +379,49 @@
     c5 = ref_arrived(0)
     relay(0)
     c5.wait()
-    align(0, True, high)
+    align(0, high, 0, True)
+    align(0, high, 1)
+    c5 = ref_arrived(1)
     relay(1)
-    c5 = ref_arrived(1)
+    c5.wait()
+    align(0, 1 - high, 0, True)
+    align(0, 1 - high, 1)
+    unit_wait(1, 1)
+    unit_wait(3, 0)
+    align(1, 0, 0)
+    align(3, 0, 0)
     relay(2)
-    c5.wait()
-    align(0, True, 1 - high)
+    align(1, 1, 0)
+    align(3, 1, 0)
     relay(3)
-    drain(e.zr.at[2], e.units.at[1, :, pl.ds(256, 512)])
-    align(1, False, 0)
-    align(1, False, 1)
-    drain(e.zr.at[5], e.units.at[3, :, pl.ds(0, 384)])
-    align(3, False, 0)
-    align(3, False, 1)
-    drain(e.zr.at[6], e.units.at[2])
-    align(2, False, 0)
-    align(2, False, 1)
-    c6 = join_start()
+    unit_wait(1, 2)
+    unit_wait(3, 3)
+    align(1, 0, 1)
+    align(3, 0, 1)
+    align(1, 1, 1)
+    align(3, 1, 1)
+    unit_wait(2, 0)
+    unit_wait(2, 1)
+    align(2, 0, 0)
+    align(2, 1, 0)
+    unit_wait(2, 3)
+    unit_wait(2, 2)
+    align(2, 0, 1)
+    c6 = join_start(0)
+    align(2, 1, 1)
+    c61 = join_start(1)
     c6.wait()
-    c7 = [normalize(0), normalize(1)]
+    c7 = [normalize(0)]
+    c7[0].wait()
+    reduce_start(0)
+    c61.wait()
+    c7 = [normalize(1)]
     for q in range(7):
         below = e.col[high, pl.ds(q, 1), :] + e.colin[high, pl.ds(q, 1), :]
         above = e.col[high, pl.ds(q + 8, 1), :] + e.colin[high, pl.ds(q + 8, 1), :]
         score_ref[:, pl.ds(q * 128, 128)] = above / below * (1.0 / TOK)
-    for block in range(2):
-        c7[block].wait()
-        reduce_start(block)
+    c7[0].wait()
+    reduce_start(1)
     drain(e.xr.at[3], e.f2.at[pl.ds(1, 15)])
     drain(e.xs.at[2], e.f2.at[pl.ds(1, 15)])
     total = e.nsum[piece_rows, :].astype(jnp.float32)
@@ -433,11 +470,12 @@
         "rw": vm((2, 256, FF_HERE), bf),
         "rt": vm((2, FF_HERE, 256), bf),
         "wr": vm((PIECE, D), bf),
+        "scl": vm((TOK, 128), f32),
         "swap": vm((PIECE, TOK), f32),
         "swin": vm((PIECE, TOK), f32),
         "refs": vm((JOINT, TOK), bf),
         "units": vm((4, TOK, FF_HERE), bf),
-        "wts": vm((JC, FF_HERE), bf),
+        "wts": vm((FF_HERE, 512), bf),
         "num": vm((JOINT, TOK), f32),
         "cs": vm((JOINT, 128), f32),
         "ws": vm((JOINT, 128), f32),
@@ -456,8 +494,9 @@
         "wshare": dma((2,)),
         "csem": dma((8,)),
         "crsem": dma((11,)),
+        "jsem": dma((4,)),
         "zs": dma((2,)),
-        "zr": dma((7,)),
+        "zr": dma((12,)),
         "xs": dma((4,)),
         "xr": dma((5,)),
     }

time: 88.6 us -> 84.6 us (0.955)
  Pallas kernels: 87.5 us -> 83.8 us
    pallas_call x1, Pallas kernels: 85.5 us -> 81.8 us  [body(): pl.pallas_call(kernel, out_shape=(jax.ShapeDtypeStruct((2, 8, PIECE, 128)...]
where the time goes in v6:
time: 84.6 us; the launch traced here: 84.4 us
  Pallas kernels  83.8 us (99%)
    pallas_call x1, Pallas kernels, body(): pl.pallas_call(kernel, out_shape=(jax.ShapeDtypeStruct((2, 8, PIECE, 128)...  81.8 us
    pallas_call x1, Pallas kernels, body(): pl.pallas_call(finish_kernel, out_shape=(jax.ShapeDtypeStruct((FF_HERE, T...  2.01 us

profile of v6, /device:TPU:17, one launch (start us, length us, event | category | flops | bytes accessed | tf_op | source)
XLA Modules:
  0.0 84.4 jit_solution(6616121520834735585)
XLA Ops:
  0.6 81.8 %soft_alignment.1 = (bf16[2,8,112,128]{3,2,1,0:T(8,128)(2,1)}, f32[1,896]{1,0:T(1,128)}) custom-call(s32[1,256]{1,0:T(1,128)} %bitcast.3, f32[1,4096]{1,0:T(1,128)} %bitcast.2, bf16[512,4096]{1,0:T(8,128)(2,1)} %table_ref.1, bf16[1,4096,896]{2,1,0:T(8,128)(2,1)} %cg_ref.1, bf16[1,4096,896]{2,1,0:T(8,128)(2,1)} %cu_ref.1, bf16[256,896]{1,0:T(8,128)(2,1)} %rg_ref.1, ...), custom_call_target="tpu_custom_call" | custom-call | tf_op jit(solution)/shard_map/soft_alignment/pallas_call | solution.py:522
  82.4 2.0 %finish.1 = (f32[896,256]{1,0:T(8,128)}, f32[1,896]{1,0:T(1,128)}) custom-call(bf16[2,8,112,128]{3,2,1,0:T(8,128)(2,1)} %get-tuple-element.4.fin_ref, f32[1,896]{1,0:T(1,128)} %get-tuple-element.5.mean_ref), custom_call_target="tpu_custom_call" | custom-call | tf_op jit(solution)/shard_map/finish/pallas_call | solution.py:534

commit v7 on v6

--- a/solution.py
+++ b/solution.py
@@ -215,48 +215,83 @@
         for d in (1, 2, 3):
             send(piece, piece, ssem.at[p], rsem.at[p, 4], me.peer(axis, d))
     share(SHARES[5])
+    def prepare(p, h, first=False):
+        off, width = PARTS[p]
+        cols = pl.ds(pl.multiple_of(h * HALF + off, 128), width)
+        v = e.fulls[p][h].astype(jnp.float32)
+        squares = v * v
+        total = squares[:, :128]
+        for o in range(128, width, 128):
+            total = total + squares[:, o : o + 128]
+        e.scl[...] = total if first else e.scl[...] + total
+        e.x[:, cols] = (v * gain_ref[:, cols]).astype(jnp.bfloat16)
+
     s6 = []
     for p in range(NP):
         drain(rsem.at[p, 4], e.r1s[p])
         drain(ssem.at[p], e.r1s[p])
         piece = e.fulls[p].at[core]
         s6.append(send(piece, piece, ssem.at[p], rsem.at[p, 5], mate))
+        prepare(p, core, p == 0)
     apart = e.wr.at[:, pl.ds(256, D - 256)]
     drain(e.wshare.at[1], apart)
     drain(e.wshare.at[0], apart)
-    for t in range(0, D, 512):
-        cols = pl.ds(t, 512)
-        e.wr[:, cols] = (e.wr[:, cols].astype(jnp.float32) * gain_ref[:, cols]).astype(jnp.bfloat16)
-
-    def ref_part(p, h):
-        off, width = PARTS[p]
-        cols = pl.ds(pl.multiple_of(h * HALF + off, 128), width)
+
+    def half_of(h):
+        return pl.ds(pl.multiple_of(h * HALF, HALF), HALF)
+
+    def ref_half(h):
         return lax.dot_general(
-            e.wr[:, cols], e.fulls[p][h], (((1,), (1,)), ((), ())), preferred_element_type=jnp.float32
+            e.wr[:, half_of(h)], e.x[:, half_of(h)], (((1,), (1,)), ((), ())), preferred_element_type=jnp.float32
         )
 
-    product = ref_part(0, core)
-    for p in range(1, NP):
-        product = product + ref_part(p, core)
+    def client_half(k, h):
+        return jnp.dot(e.x[:, half_of(h)], e.w[k, half_of(h), :], preferred_element_type=jnp.float32)
+
+    e.swap[...] = ref_half(core)
+    for k in range(2):
+        wload[0, k].wait()
+    e.acc[0] = client_half(0, core)
     for p in range(NP):
         s6[p].wait()
-        product = product + ref_part(p, other)
-    e.swap[...] = product
+        prepare(p, other)
+    e.swap[...] = e.swap[...] + ref_half(other)
     c3 = send(e.swap, e.swin, e.csem.at[1], e.crsem.at[4], mate)
-    for t in range(0, TOK, 32):
-        total = jnp.zeros((32, 1), jnp.float32)
-        for p in range(NP):
-            for h in range(2):
-                v = e.fulls[p][h, pl.ds(t, 32), :].astype(jnp.float32)
-                total = total + jnp.sum(v * v, axis=1, keepdims=True)
-        scale = lax.rsqrt(total * (1.0 / D) + 1e-05)
-        e.scl[pl.ds(t, 32), :] = jnp.broadcast_to(scale, (32, 128))
-        for p, (off, width) in enumerate(PARTS):
-            for h in range(2):
-                v = e.fulls[p][h, pl.ds(t, 32), :].astype(jnp.float32)
-                cols = pl.ds(h * HALF + off, width)
-                e.x[pl.ds(t, 32), cols] = (v * scale * gain_ref[:, cols]).astype(jnp.bfloat16)
-
+    scale = lax.rsqrt(jnp.sum(e.scl[...], axis=1, keepdims=True) * (1.0 / D) + 1e-05)
+    e.scl[...] = jnp.broadcast_to(scale, (TOK, 128))
+
+    def client_block(q):
+        start, width = SPANS[q]
+        for k in range(2):
+            if q > 0:
+                wload[q, k].wait()
+        if q == 0:
+            g = e.acc[0] + client_half(0, other)
+            u = jnp.dot(e.x[...], e.w[1], preferred_element_type=jnp.float32)
+        elif q < 3:
+            g = jnp.dot(e.x[...], e.w[q * 2], preferred_element_type=jnp.float32)
+            u = jnp.dot(e.x[...], e.w[q * 2 + 1], preferred_element_type=jnp.float32)
+        else:
+            both = jnp.dot(e.x[...], e.w[6], preferred_element_type=jnp.float32)
+            g, u = both[:, :128], both[:, 128:]
+        scales = jnp.concatenate([e.scl[...]] * (width // 128), axis=1)
+        g, u = g * scales, u * scales
+        cols = pl.ds(start, width)
+        e.units[0, :, cols] = spread(gated(g, u), 0)
+        mine = e.units.at[0, :, cols]
+        send(mine, e.units.at[1, :, cols], e.zs.at[0], e.zr.at[q], me.peer("z", 1))
+        send(mine, e.units.at[3, :, cols], e.zs.at[0], e.zr.at[8 + q], me.peer("z", 3))
+
+    def relay(q):
+        slot, step = (1, 1) if q in (0, 3) else (3, 3)
+        piece = e.units.at[slot, :, pl.ds(*SPANS[q])]
+        drain(e.zr.at[q if slot == 1 else 8 + q], piece)
+        send(piece, e.units.at[2, :, pl.ds(*SPANS[q])], e.zs.at[1], e.zr.at[4 + q], me.peer("z", step))
+
+    def unit_wait(slot, q):
+        drain(e.zr.at[(slot - 1) * 4 + q], e.units.at[slot, :, pl.ds(*SPANS[q])])
+
+    client_block(0)
     c3.wait()
     scale_row = jnp.concatenate(
         [jnp.sum(jnp.where(eye, e.scl[pl.ds(t, 128), :], 0.0), axis=0, keepdims=True) for t in (0, 128)], axis=1
@@ -267,53 +302,36 @@
     g = jnp.where(lead, mine, theirs)
     u = jnp.where(lead, theirs, mine)
     high = me.y // 2
+    half = pl.ds(pl.multiple_of(core * 128, 128), 128)
+
+    def ref_piece(block, dx, f):
+        return e.refs.at[rows(block * FF_HERE + me.plane_piece(dx, f) * PIECE, PIECE), half]
+
     piece_rows = rows(high * FF_HERE + here * PIECE, PIECE)
-    half = pl.ds(pl.multiple_of(core * 128, 128), 128)
     piece_std = spread(gated(g, u), 1)
     e.refs[piece_rows, half] = jnp.where(lead, piece_std[:, :128], piece_std[:, 128:])
-    piece = e.refs.at[piece_rows, half]
-    for dx, f in RING8:
-        send(piece, piece, e.xs.at[0], e.xr.at[0], me.plane_peer(dx, f, 0))
-    for dx in range(4):
-        for f in range(2):
-            send(piece, piece, e.xs.at[1], e.xr.at[2], me.plane_peer(dx, f, 1))
-
-    def client_block(q):
-        start, width = SPANS[q]
-        for k in range(2):
-            wload[q, k].wait()
-        if q < 3:
-            g = jnp.dot(e.x[...], e.w[q * 2], preferred_element_type=jnp.float32)
-            u = jnp.dot(e.x[...], e.w[q * 2 + 1], preferred_element_type=jnp.float32)
-        else:
-            both = jnp.dot(e.x[...], e.w[6], preferred_element_type=jnp.float32)
-            g, u = both[:, :128], both[:, 128:]
-        cols = pl.ds(start, width)
-        e.units[0, :, cols] = spread(gated(g, u), 0)
-        mine = e.units.at[0, :, cols]
-        send(mine, e.units.at[1, :, cols], e.zs.at[0], e.zr.at[q], me.peer("z", 1))
-        send(mine, e.units.at[3, :, cols], e.zs.at[0], e.zr.at[8 + q], me.peer("z", 3))
-
-    def relay(q):
-        slot, step = (1, 1) if q in (0, 3) else (3, 3)
-        piece = e.units.at[slot, :, pl.ds(*SPANS[q])]
-        drain(e.zr.at[q if slot == 1 else 8 + q], piece)
-        send(piece, e.units.at[2, :, pl.ds(*SPANS[q])], e.zs.at[1], e.zr.at[4 + q], me.peer("z", step))
-
-    def unit_wait(slot, q):
-        drain(e.zr.at[(slot - 1) * 4 + q], e.units.at[slot, :, pl.ds(*SPANS[q])])
-
-    client_block(0)
+    piece = ref_piece(high, 0, 0)
+    for n, (dx, f) in enumerate(RING8, 1):
+        send(piece, piece, e.xs.at[0], e.xr.at[n], me.plane_peer(dx, f, 0))
+    for n, (dx, f) in enumerate([(0, 0)] + RING8):
+        send(piece, piece, e.xs.at[1], e.xr.at[8 + n], me.plane_peer(dx, f, 1))
+    send(piece, piece, e.csem.at[2], e.crsem.at[5], mate)
     client_block(1)
     client_block(2)
     client_block(3)
     def ref_arrived(k):
-        came = e.refs.at[pl.ds(0, (7 + k) * PIECE), half]
-        drain(e.xr.at[(0, 2)[k]], came)
-        drain(e.xs.at[k], came)
         block = high if k == 0 else 1 - high
-        part = e.refs.at[rows(block * FF_HERE, FF_HERE), half]
-        return send(part, part, e.csem.at[2 + k], e.crsem.at[5 + k], mate)
+        for n, (dx, f) in enumerate([(0, 0)] + RING8):
+            if k == 1 or n > 0:
+                came = ref_piece(block, (4 - dx) % 4, f)
+                drain(e.xr.at[8 * k + n], came)
+                send(came, came, e.csem.at[2 + k], e.crsem.at[5 + k], mate)
+
+    def mate_done(k):
+        part = e.refs.at[pl.ds(0, FF_HERE), half]
+        drain(e.crsem.at[5 + k], part)
+        drain(e.csem.at[2 + k], part)
+        drain(e.xs.at[k], e.refs.at[pl.ds(0, (7 + k) * PIECE), half])
 
     def align(slot, block, k, first=False):
         left, wide = ((0, 512), (512, 384))[k]
@@ -368,7 +386,7 @@
                 n = hop * 8 + dx * 2 + f
                 src = e.nsum.at[rows(block * FF_HERE + me.plane_piece(dx, f) * PIECE, PIECE)]
                 copy = pltpu.make_async_remote_copy(
-                    src_ref=src, dst_ref=e.f2.at[n], send_sem=e.xs.at[2], recv_sem=e.xr.at[3],
+                    src_ref=src, dst_ref=e.f2.at[n], send_sem=e.xs.at[2], recv_sem=e.xr.at[0],
                     device_id=me.plane_peer(dx, f, hop), device_id_type=MESH,
                 )
                 if dx == 0 and f == 0:
@@ -376,23 +394,23 @@
                 else:
                     copy.start()
 
-    c5 = ref_arrived(0)
+    ref_arrived(0)
     relay(0)
-    c5.wait()
+    mate_done(0)
     align(0, high, 0, True)
     align(0, high, 1)
-    c5 = ref_arrived(1)
     relay(1)
-    c5.wait()
+    unit_wait(1, 1)
+    unit_wait(3, 0)
+    ref_arrived(1)
+    align(1, high, 0)
+    align(3, high, 0)
+    mate_done(1)
     align(0, 1 - high, 0, True)
     align(0, 1 - high, 1)
-    unit_wait(1, 1)
-    unit_wait(3, 0)
-    align(1, 0, 0)
-    align(3, 0, 0)
     relay(2)
-    align(1, 1, 0)
-    align(3, 1, 0)
+    align(1, 1 - high, 0)
+    align(3, 1 - high, 0)
     relay(3)
     unit_wait(1, 2)
     unit_wait(3, 3)
@@ -412,32 +430,35 @@
     c61 = join_start(1)
     c6.wait()
     c7 = [normalize(0)]
-    c7[0].wait()
-    reduce_start(0)
     c61.wait()
-    c7 = [normalize(1)]
+    c7.append(normalize(1))
     for q in range(7):
         below = e.col[high, pl.ds(q, 1), :] + e.colin[high, pl.ds(q, 1), :]
         above = e.col[high, pl.ds(q + 8, 1), :] + e.colin[high, pl.ds(q + 8, 1), :]
         score_ref[:, pl.ds(q * 128, 128)] = above / below * (1.0 / TOK)
-    c7[0].wait()
-    reduce_start(1)
-    drain(e.xr.at[3], e.f2.at[pl.ds(1, 15)])
+    for block in range(2):
+        c7[block].wait()
+        reduce_start(block)
+    drain(e.xr.at[0], e.f2.at[pl.ds(1, 15)])
     drain(e.xs.at[2], e.f2.at[pl.ds(1, 15)])
     total = e.nsum[piece_rows, :].astype(jnp.float32)
     for n in range(1, 16):
         total = total + e.f2[n].astype(jnp.float32)
     mine = e.fin.at[core, here]
     mine[...] = total.astype(jnp.bfloat16)
-    for dx, f in RING8:
-        send(mine, mine, e.xs.at[3], e.xr.at[4], me.plane_peer(dx, f, 0))
-    drain(e.xr.at[4], e.fin.at[0, pl.ds(1, 7)])
+    send(mine, mine, e.csem.at[7], e.crsem.at[10], mate)
+    for n, (dx, f) in enumerate(RING8):
+        send(mine, mine, e.xs.at[3], e.xr.at[16 + n], me.plane_peer(dx, f, 0))
+    for n, (dx, f) in enumerate(RING8):
+        came = e.fin.at[core, me.plane_piece(4 - dx, f)]
+        drain(e.xr.at[16 + n], came)
+        send(came, came, e.csem.at[7], e.crsem.at[10], mate)
     drain(e.xs.at[3], e.fin.at[0, pl.ds(1, 7)])
-    c10 = send(e.fin.at[core], e.fin.at[core], e.csem.at[7], e.crsem.at[10], mate)
     for _ in range(2):
         drain(e.zs.at[0], e.units.at[0])
     drain(e.zs.at[1], e.units.at[2])
-    c10.wait()
+    drain(e.crsem.at[10], e.fin.at[0])
+    drain(e.csem.at[7], e.fin.at[0])
     fin_ref[...] = e.fin[...]
 
 
@@ -470,6 +491,7 @@
         "rw": vm((2, 256, FF_HERE), bf),
         "rt": vm((2, FF_HERE, 256), bf),
         "wr": vm((PIECE, D), bf),
+        "acc": vm((1, TOK, 256), f32),
         "scl": vm((TOK, 128), f32),
         "swap": vm((PIECE, TOK), f32),
         "swin": vm((PIECE, TOK), f32),
@@ -498,7 +520,7 @@
         "zs": dma((2,)),
         "zr": dma((12,)),
         "xs": dma((4,)),
-        "xr": dma((5,)),
+        "xr": dma((23,)),
     }
 
 

time: 84.6 us -> 83.8 us (level)
  no operation moved by 1% of the time
where the time goes in v7:
time: 83.8 us; the launch traced here: 83.6 us
  Pallas kernels  83 us (99%)
    pallas_call x1, Pallas kernels, body(): pl.pallas_call(kernel, out_shape=(jax.ShapeDtypeStruct((2, 8, PIECE, 128)...  81 us
    pallas_call x1, Pallas kernels, body(): pl.pallas_call(finish_kernel, out_shape=(jax.ShapeDtypeStruct((FF_HERE, T...  2.01 us

profile of v7, /device:TPU:17, one launch (start us, length us, event | category | flops | bytes accessed | tf_op | source)
XLA Modules:
  0.0 83.6 jit_solution(7901700528283511635)
XLA Ops:
  0.6 81.0 %soft_alignment.1 = (bf16[2,8,112,128]{3,2,1,0:T(8,128)(2,1)}, f32[1,896]{1,0:T(1,128)}) custom-call(s32[1,256]{1,0:T(1,128)} %bitcast.3, f32[1,4096]{1,0:T(1,128)} %bitcast.2, bf16[512,4096]{1,0:T(8,128)(2,1)} %table_ref.1, bf16[1,4096,896]{2,1,0:T(8,128)(2,1)} %cg_ref.1, bf16[1,4096,896]{2,1,0:T(8,128)(2,1)} %cu_ref.1, bf16[256,896]{1,0:T(8,128)(2,1)} %rg_ref.1, ...), custom_call_target="tpu_custom_call" | custom-call | tf_op jit(solution)/shard_map/soft_alignment/pallas_call | solution.py:544
  81.6 2.0 %finish.1 = (f32[896,256]{1,0:T(8,128)}, f32[1,896]{1,0:T(1,128)}) custom-call(bf16[2,8,112,128]{3,2,1,0:T(8,128)(2,1)} %get-tuple-element.4.fin_ref, f32[1,896]{1,0:T(1,128)} %get-tuple-element.5.mean_ref), custom_call_target="tpu_custom_call" | custom-call | tf_op jit(solution)/shard_map/finish/pallas_call | solution.py:556

commit v8 on v7

--- a/solution.py
+++ b/solution.py
@@ -11,7 +11,7 @@
 TOK = 256
 D = 4096
 HALF = D // 2
-PARTS = ((0, 384), (384, 384), (768, 384), (1152, 384), (1536, 256), (1792, 256))
+PARTS = ((0, 384), (384, 384), (768, 384), (1152, 256), (1408, 256), (1664, 384))
 ORDERS = ("xyz", "yzx", "zxy") * 2
 NP = len(PARTS)
 
@@ -72,6 +72,7 @@
 SHARES = (4, 3, 3, 3, 2, 0)
 SPANS = ((0, 256), (256, 256), (512, 256), (768, 128))
 RING8 = [(dx, f) for dx in range(4) for f in range(2)][1:]
+STEPS = 2
 CROSS = [(dx, f, c) for dx in range(4) for f in range(2) for c in range(2)][1:]
 RING16 = [(dx, f, h) for h in range(2) for dx in range(4) for f in range(2)][1:]
 EXP_SCALE = sharpness / TOK * 1.4426950408889634
@@ -88,7 +89,7 @@
     return g / (1.0 + jnp.exp(-g)) * u
 
 
-def kernel(ids_ref, gain_ref, table_ref, cg_ref, cu_ref, rg_ref, ru_ref, fin_ref, score_ref, *scratch):
+def kernel(ids_hbm, gain_hbm, table_ref, cg_ref, cu_ref, rg_ref, ru_ref, fin_ref, score_ref, *scratch):
     e = Refs(scratch)
     me = Place()
     core, other = me.core, 1 - me.core
@@ -96,6 +97,12 @@
     client = lax.axis_index("client")
     ssem, rsem = e.ssem, e.rsem
 
+    ids_ref, gain_ref = e.ids, e.gain
+    small = [
+        pltpu.make_async_copy(ids_hbm, ids_ref, e.rwsem.at[1]),
+        pltpu.make_async_copy(gain_hbm, gain_ref, e.rwsem.at[2]),
+    ]
+    small[0].start()
     def table_load(k):
         half = other if k < 4 else core
         at = pl.multiple_of(half * HALF + k % 4 * 512, 512)
@@ -107,6 +114,7 @@
     for t, src in enumerate((rg_ref, ru_ref)):
         pltpu.make_async_copy(src, e.rw.at[t], e.rwsem.at[0]).start()
     loads += [table_load(k) for k in range(4, 8)]
+    small[1].start()
 
     barrier = pltpu.get_barrier_semaphore()
     peers = [me.plane_peer(*r) for r in RING16] + [me.peer("z", d) for d in (1, 2, 3)] + [mate]
@@ -117,6 +125,7 @@
     eye = lax.broadcasted_iota(jnp.int32, (128, 128), 0) == lax.broadcasted_iota(jnp.int32, (128, 128), 1)
     start = (client * 8 + lax.axis_index("unit")) * 512
     table_rows = (start + lax.broadcasted_iota(jnp.int32, (1, 512), 1)).astype(jnp.float32)
+    small[0].wait()
     for t in range(2):
         wide = ids_ref[:, pl.ds(t * 128, 128)].astype(jnp.float32)
         tall = jnp.sum(jnp.where(eye, wide, 0.0), axis=1, keepdims=True)
@@ -166,6 +175,7 @@
         load.start()
         wload[3, k] = load
 
+    small[1].wait()
     for k in range(4):
         sent[k].wait_recv()
         e.accs[:, chunks[k]] = e.accs[:, chunks[k]] + e.cins[:, chunks[k]]
@@ -311,21 +321,18 @@
     piece_std = spread(gated(g, u), 1)
     e.refs[piece_rows, half] = jnp.where(lead, piece_std[:, :128], piece_std[:, 128:])
     piece = ref_piece(high, 0, 0)
-    for n, (dx, f) in enumerate(RING8, 1):
-        send(piece, piece, e.xs.at[0], e.xr.at[n], me.plane_peer(dx, f, 0))
-    for n, (dx, f) in enumerate([(0, 0)] + RING8):
-        send(piece, piece, e.xs.at[1], e.xr.at[8 + n], me.plane_peer(dx, f, 1))
-    send(piece, piece, e.csem.at[2], e.crsem.at[5], mate)
+    for dx, f in RING8:
+        send(piece, piece, e.xs.at[0], e.xr.at[0], me.plane_peer(dx, f, 0))
+    for dx, f in [(0, 0)] + RING8:
+        send(piece, piece, e.xs.at[1], e.xr.at[1], me.plane_peer(dx, f, 1))
     client_block(1)
     client_block(2)
     client_block(3)
     def ref_arrived(k):
         block = high if k == 0 else 1 - high
-        for n, (dx, f) in enumerate([(0, 0)] + RING8):
-            if k == 1 or n > 0:
-                came = ref_piece(block, (4 - dx) % 4, f)
-                drain(e.xr.at[8 * k + n], came)
-                send(came, came, e.csem.at[2 + k], e.crsem.at[5 + k], mate)
+        drain(e.xr.at[k], e.refs.at[pl.ds(0, (7 + k) * PIECE), half])
+        part = e.refs.at[rows(block * FF_HERE, FF_HERE), half]
+        send(part, part, e.csem.at[2 + k], e.crsem.at[5 + k], mate)
 
     def mate_done(k):
         part = e.refs.at[pl.ds(0, FF_HERE), half]
@@ -386,7 +393,7 @@
                 n = hop * 8 + dx * 2 + f
                 src = e.nsum.at[rows(block * FF_HERE + me.plane_piece(dx, f) * PIECE, PIECE)]
                 copy = pltpu.make_async_remote_copy(
-                    src_ref=src, dst_ref=e.f2.at[n], send_sem=e.xs.at[2], recv_sem=e.xr.at[0],
+                    src_ref=src, dst_ref=e.f2.at[n], send_sem=e.xs.at[2], recv_sem=e.xr.at[2],
                     device_id=me.plane_peer(dx, f, hop), device_id_type=MESH,
                 )
                 if dx == 0 and f == 0:
@@ -439,20 +446,17 @@
     for block in range(2):
         c7[block].wait()
         reduce_start(block)
-    drain(e.xr.at[0], e.f2.at[pl.ds(1, 15)])
+    drain(e.xr.at[2], e.f2.at[pl.ds(1, 15)])
     drain(e.xs.at[2], e.f2.at[pl.ds(1, 15)])
     total = e.nsum[piece_rows, :].astype(jnp.float32)
     for n in range(1, 16):
         total = total + e.f2[n].astype(jnp.float32)
     mine = e.fin.at[core, here]
     mine[...] = total.astype(jnp.bfloat16)
-    send(mine, mine, e.csem.at[7], e.crsem.at[10], mate)
-    for n, (dx, f) in enumerate(RING8):
-        send(mine, mine, e.xs.at[3], e.xr.at[16 + n], me.plane_peer(dx, f, 0))
-    for n, (dx, f) in enumerate(RING8):
-        came = e.fin.at[core, me.plane_piece(4 - dx, f)]
-        drain(e.xr.at[16 + n], came)
-        send(came, came, e.csem.at[7], e.crsem.at[10], mate)
+    for dx, f in RING8:
+        send(mine, mine, e.xs.at[3], e.xr.at[3], me.plane_peer(dx, f, 0))
+    drain(e.xr.at[3], e.fin.at[0, pl.ds(1, 7)])
+    send(e.fin.at[core], e.fin.at[core], e.csem.at[7], e.crsem.at[10], mate)
     drain(e.xs.at[3], e.fin.at[0, pl.ds(1, 7)])
     for _ in range(2):
         drain(e.zs.at[0], e.units.at[0])
@@ -463,7 +467,7 @@
 
 
 def finish_kernel(fin_ref, mean_ref, merged_ref, score_ref):
-    for s in range(8):
+    for s in range(8 // STEPS):
         for h in range(2):
             merged_ref[pl.ds(s * PIECE, PIECE), pl.ds(h * 128, 128)] = fin_ref[h, s].astype(jnp.float32) * (1.0 / 16)
     score_ref[...] = mean_ref[...]
@@ -485,6 +489,8 @@
         "a2s": [vm((16, w), bf) for w in widths],
         "r3s": [vm((3, 16, w), bf) for w in widths],
         "fulls": [vm((2, TOK, w), bf) for w in widths],
+        "ids": vm((1, TOK), jnp.int32),
+        "gain": vm((1, D), f32),
         "pick": vm((TOK, 512), bf),
         "x": vm((TOK, D), bf),
         "w": vm((7, D, 256), bf),
@@ -512,7 +518,7 @@
         "ssem": dma((NP,)),
         "rsem": dma((NP, 6)),
         "wsem": dma((8,)),
-        "rwsem": dma((1,)),
+        "rwsem": dma((3,)),
         "wshare": dma((2,)),
         "csem": dma((8,)),
         "crsem": dma((11,)),
@@ -520,7 +526,7 @@
         "zs": dma((2,)),
         "zr": dma((12,)),
         "xs": dma((4,)),
-        "xr": dma((23,)),
+        "xr": dma((4,)),
     }
 
 
@@ -547,7 +553,7 @@
             jax.ShapeDtypeStruct((2, 8, PIECE, 128), jnp.bfloat16),
             jax.ShapeDtypeStruct((1, FF_HERE), f32),
         ),
-        in_specs=[vmem, vmem, hbm, hbm, hbm, hbm, hbm],
+        in_specs=[hbm] * 7,
         out_specs=(vmem, vmem),
         scratch_shapes=shapes,
         compiler_params=pltpu.CompilerParams(collective_id=0, has_side_effects=True, vmem_limit_bytes=60 << 20),
@@ -556,8 +562,15 @@
     return pl.pallas_call(
         finish_kernel,
         out_shape=(jax.ShapeDtypeStruct((FF_HERE, TOK), f32), jax.ShapeDtypeStruct((1, FF_HERE), f32)),
-        in_specs=[vmem, vmem],
-        out_specs=(vmem, vmem),
+        grid=(STEPS,),
+        in_specs=[
+            pl.BlockSpec((2, 8 // STEPS, PIECE, 128), lambda t: (0, t, 0, 0)),
+            pl.BlockSpec((1, FF_HERE), lambda t: (0, 0)),
+        ],
+        out_specs=(
+            pl.BlockSpec((FF_HERE // STEPS, TOK), lambda t: (t, 0)),
+            pl.BlockSpec((1, FF_HERE), lambda t: (0, 0)),
+        ),
         name="finish",
     )(fin, mean)
 

time: 83.8 us -> 82.6 us (0.986)
  Pallas kernels: 83 us -> 81.8 us
    pallas_call x1, Pallas kernels: 81 us -> 79.9 us  [body(): pl.pallas_call(kernel, out_shape=(jax.ShapeDtypeStruct((2, 8, PIECE, 128)...]
where the time goes in v8:
time: 82.6 us; the launch traced here: 82.5 us
  Pallas kernels  81.8 us (99%)
    pallas_call x1, Pallas kernels, body(): pl.pallas_call(kernel, out_shape=(jax.ShapeDtypeStruct((2, 8, PIECE, 128)...  79.9 us
    pallas_call x1, Pallas kernels, body(): pl.pallas_call(finish_kernel, out_shape=(jax.ShapeDtypeStruct((FF_HERE, T...  1.92 us

profile of v8, /device:TPU:17, one launch (start us, length us, event | category | flops | bytes accessed | tf_op | source)
XLA Modules:
  0.0 82.5 jit_solution(16651818219941655803)
XLA Ops:
  0.6 79.9 %soft_alignment.1 = (bf16[2,8,112,128]{3,2,1,0:T(8,128)(2,1)}, f32[1,896]{1,0:T(1,128)}) custom-call(s32[1,256]{1,0:T(1,128)} %bitcast.3, f32[1,4096]{1,0:T(1,128)} %bitcast.2, bf16[512,4096]{1,0:T(8,128)(2,1)} %table_ref.1, bf16[1,4096,896]{2,1,0:T(8,128)(2,1)} %cg_ref.1, bf16[1,4096,896]{2,1,0:T(8,128)(2,1)} %cu_ref.1, bf16[256,896]{1,0:T(8,128)(2,1)} %rg_ref.1, ...), custom_call_target="tpu_custom_call" | custom-call | tf_op jit(solution)/shard_map/soft_alignment/pallas_call | solution.py:550
  80.6 1.9 %finish.1 = (f32[896,256]{1,0:T(8,128)}, f32[1,896]{1,0:T(1,128)}) custom-call(bf16[2,8,112,128]{3,2,1,0:T(8,128)(2,1)} %get-tuple-element.4.fin_ref, f32[1,896]{1,0:T(1,128)} %get-tuple-element.5.mean_ref), custom_call_target="tpu_custom_call" | custom-call | tf_op jit(solution)/shard_map/finish/pallas_call | solution.py:562
